TPU v7x, 768 devices: a whole 4x8x12 slice. The times are simulated.
768 devices in a mesh: fsdp: 96 (over y_hi, z, core), seq: 8 (over y_lo, x).
Axes of the slice: x: 4, y: 8 (y_hi: 4, y_lo: 2; y = y_hi * 2 + y_lo), z: 12, core: 2. Of those that a mesh axis runs over, the one named last changes fastest.
Arguments:
- query_proj: bfloat16 [96, 1024, 3072], P('fsdp', 'seq'), may hold values from -6 to 6
- key_proj: bfloat16 [96, 1024, 3072], P('fsdp', 'seq'), may hold values from 0 to 5
- value_proj: bfloat16 [96, 1024, 3072], P('fsdp', 'seq'), may hold values from 0 to 5
- filters: float32 [3072, 128], P('fsdp'), may hold values from -8 to 8
Outputs:
- response: bfloat16 [96, 1024, 3072], P('fsdp', 'seq')
All inputs are finite; a program needn't handle non-finite values.
Results may differ from a plain program's by a relative error of at most 0.012.
Values may be sent and summed in bfloat16 or wider, within the bound.
No kernel may reach another device: no remote copies, remote signals or barrier semaphores. Data moves between devices by JAX's collectives and lax.ppermute only.
A program may use at most 32 MiB of HBM per device.

v0:
```python
import jax
import jax.numpy as jnp
from jax import lax
from jax.sharding import PartitionSpec as P


def passed_along(shard, axis, by):
    peers = lax.axis_size(axis)
    pairs = [(i, i + by) for i in range(peers) if 0 <= i + by < peers]
    return lax.ppermute(shard, axis, pairs)


def depthwise(padded, taps):
    kernel = jnp.transpose(taps[:, ::-1])[:, None, :]
    return lax.conv_general_dilated(
        padded,
        kernel,
        (1,),
        "VALID",
        dimension_numbers=("NWC", "WIO", "NWC"),
        feature_group_count=taps.shape[0],
        precision=lax.Precision.HIGHEST,
    )


def per_device(query_proj, key_proj, value_proj, filters):
    mixed = (key_proj.astype(jnp.float32) * value_proj.astype(jnp.float32)).astype(jnp.bfloat16)
    span = filters.shape[1] - 1
    earlier = passed_along(mixed[:, mixed.shape[1] - span :, :], "seq", 1)
    padded = jnp.concatenate([earlier, mixed], axis=1).astype(jnp.float32)
    filtered = depthwise(padded, lax.all_gather(filters, "fsdp", axis=0, tiled=True))
    return (query_proj.astype(jnp.float32) * filtered).astype(jnp.bfloat16)


def solution(mesh):
    in_specs = (
        P("fsdp", "seq", None),
        P("fsdp", "seq", None),
        P("fsdp", "seq", None),
        P("fsdp", None),
    )
    out_specs = P("fsdp", "seq", None)
    return jax.shard_map(
        per_device, mesh=mesh, in_specs=in_specs, out_specs=out_specs, check_vma=False
    )
```

profile of v0, /device:TPU:1, one launch (start us, length us, event | category | flops | bytes accessed | tf_op | source)
XLA Modules:
  0.0 176.5 jit_solution(10630649399223149645)
XLA Ops:
  6.5 0.0 all-gather.2.cloned.1.call-start
  6.5 0.7 all-gather.2.cloned.1.call-update
  7.3 1.6 multiply_convert_fusion
  8.8 0.2 slice.4
  9.0 4.0 %collective-permute-start = (bf16[1,127,3072]{2,1,0:T(8,128)(2,1)S(1)}, bf16[1,127,3072]{2,1,0:T(8,128)(2,1)S(1)}, u32[]{:S(2)}, u32[]{:S(2)}) collective-permute-start(bf16[1,127,3072]{2,1,0:T(8,128)(2,1)S(1)} %slice.4), channel_id=1, source_target_pairs={{0,1},{1,2},{2,3},{3,4},{4,5},{5,6},{6,7},{8,9},{9,10},{10,11},{11... | collective-permute-start | bytes 2340872 | tf_op jit(solution)/shard_map/ppermute | solution.py:10
  13.0 9.3 %collective-permute-done = bf16[1,127,3072]{2,1,0:T(8,128)(2,1)S(1)} collective-permute-done((bf16[1,127,3072]{2,1,0:T(8,128)(2,1)S(1)}, bf16[1,127,3072]{2,1,0:T(8,128)(2,1)S(1)}, u32[]{:S(2)}, u32[]{:S(2)}) %collective-permute-start) | collective-permute-done | bytes 780320 | tf_op jit(solution)/shard_map/ppermute | solution.py:10
  22.3 0.2 pad_maximum_fusion
  22.5 113.4 %all-gather.2.cloned.1.call-done = f32[3072,128]{1,0:T(8,128)} async-done(((f32[32,128]{1,0:T(8,128)}), f32[3072,128]{1,0:T(8,128)}) %all-gather.2.cloned.1.call-update) | async-done | bytes 1572880 | tf_op jit(solution)/shard_map/all_gather | solution.py:31
  135.9 11.2 %rev.3 = f32[3072,128]{1,0:T(8,128)S(1)} reverse(f32[3072,128]{1,0:T(8,128)} %all-gather.2.cloned.1.call-done), dimensions={1} | reverse | bytes 3145728 | tf_op jit(solution)/shard_map/rev | solution.py:14
  147.2 3.1 %copy.18 = f32[128,1,3072]{2,1,0:T(1,128)} copy(f32[128,1,3072]{0,2,1:T(8,128)S(1)} %bitcast.4) | data formatting | bytes 3145728 | tf_op jit(solution)/shard_map/broadcast_in_dim | solution.py:14
  150.3 0.0 copy-start
  150.3 18.1 %fusion = f32[1,128,3072]{2,0,1:T(1,128)S(1)} fusion(f32[128,1,3072]{2,1,0:T(1,128)} %copy.18, bf16[1,255,3072]{2,1,0:T(8,128)(2,1)S(1)} %pad_maximum_fusion), kind=kOutput, calls=%fused_computation | convolution fusion | flops 603979776 | bytes 4712448 | tf_op jit(solution)/shard_map/conv_general_dilated | solution.py:15
  168.4 0.0 copy-done
  168.4 1.2 fusion.2
Async XLA Ops:
  6.5 129.4 %all-gather.2.cloned.1.call-start = ((), (), s32[]{:S(2)}) async-start(), calls=%async_computation | async-start | bytes 1589248 | tf_op jit(solution)/shard_map/all_gather | solution.py:31
  9.0 13.3 %collective-permute-start = (bf16[1,127,3072]{2,1,0:T(8,128)(2,1)S(1)}, bf16[1,127,3072]{2,1,0:T(8,128)(2,1)S(1)}, u32[]{:S(2)}, u32[]{:S(2)}) collective-permute-start(bf16[1,127,3072]{2,1,0:T(8,128)(2,1)S(1)} %slice.4), channel_id=1, source_target_pairs={{0,1},{1,2},{2,3},{3,4},{4,5},{5,6},{6,7},{8,9},{9,10},{10,11},{11... | collective-permute-start | bytes 2340872 | tf_op jit(solution)/shard_map/ppermute | solution.py:10
  150.3 18.1 %copy-start = (bf16[1,128,3072]{2,1,0:T(8,128)(2,1)S(1)}, bf16[1,128,3072]{2,1,0:T(8,128)(2,1)}, u32[]{:S(2)}) copy-start(bf16[1,128,3072]{2,1,0:T(8,128)(2,1)} %param.4) | copy-start | bytes 2359300
Sparse Core Ops, SparseCore 0:
  11.0 124.9 all-gather.1
where the time goes:
time: 177 us; the launch traced here: 176 us
  waiting for transfers between devices  123 us (69%)
  matrix products  18.1 us (10%)
  local copies, waits for them, and re-layouts  14.5 us (8%)
  between operations  13.4 us (8%)
  starting transfers between devices  3.98 us (2%)
  other arithmetic  3.01 us (2%)
    all_gather x1, waiting for transfers between devices, per_device(): lax.all_gather(filters, 'fsdp', axis=0, tiled=True)  113 us
    conv_general_dilated x1, matrix products, depthwise(): lax.conv_general_dilated(padded, kernel, (1,), 'VALID', dimension_numbers...  18.1 us
    rev x1, local copies, waits for them, and re-layouts, depthwise(): kernel = jnp.transpose(taps[:, ::-1])[:, None, :]  11.2 us
    ppermute x1, waiting for transfers between devices, passed_along(): return lax.ppermute(shard, axis, pairs)  9.28 us
    ppermute x1, starting transfers between devices, passed_along(): return lax.ppermute(shard, axis, pairs)  3.98 us
  transfers between devices with their start and end apart: 2, of which 2 were waited for; matrix products, arithmetic and copies ran while one was open for 1% of the time, Pallas kernels for 0%

commit v1 on v0

v1 whole, which is shorter than its diff:
```python
import functools

import jax
import jax.numpy as jnp
import numpy as np
from jax import lax
from jax.experimental import pallas as pl
from jax.experimental.pallas import tpu as pltpu
from jax.sharding import PartitionSpec as P

WIRE = jnp.float16
SCALE = 4096.0


def split(x):
    x = np.asarray(x, np.float32)
    hi = x.astype(jnp.bfloat16)
    return hi, (x - hi.astype(np.float32)).astype(jnp.bfloat16)


def transforms(taps):
    n = 2 * taps
    angle = 2 * np.pi * np.outer(np.arange(taps) + 0.5, np.arange(n)) / n
    forward = np.concatenate([np.cos(angle), -np.sin(angle)])
    inverse = np.concatenate([np.cos(angle), -np.sin(angle)]).T[taps:] / taps
    fh, fl = split(forward)
    gh, gl = split(inverse / SCALE)
    return np.concatenate([fh, fl]), np.concatenate([gh, gl])


def rows_of(ref):
    both = jnp.concatenate([ref[0], ref[1]], axis=1)
    return both.reshape(-1, both.shape[-1])


def conv_kernel(prev_ref, cur_ref, query_ref, wh_ref, wl_ref, f_ref, g_ref, out_ref):
    f32 = jnp.float32
    half, taps = f_ref.shape[0] // 2, cur_ref.shape[1]
    dot = functools.partial(jnp.dot, preferred_element_type=f32)
    f = f_ref[...]
    window = jnp.concatenate([prev_ref[0], cur_ref[0]], axis=0)
    x = dot(f, window)
    x = x[:half] + x[half:]
    nt = functools.partial(
        lax.dot_general, dimension_numbers=(((1,), (1,)), ((), ())), preferred_element_type=f32
    )
    h = nt(f[:, :taps], rows_of(wh_ref))
    h = h[:half] + h[half:] + nt(f[:half, :taps], rows_of(wl_ref))
    xr, xi, hr, hi = x[:taps], x[taps:], h[:taps], h[taps:]
    p = jnp.concatenate([xr * hr - xi * hi, xr * hi + xi * hr], axis=0)
    ph = p.astype(jnp.bfloat16)
    plo = (p - ph.astype(f32)).astype(jnp.bfloat16)
    g = g_ref[...]
    y = dot(g, ph)
    y = y[:taps] + y[taps:] + dot(g[:taps], plo)
    out_ref[0] = (query_ref[0].astype(f32) * y).astype(out_ref.dtype)


def filtered_gate(prev, cur, query, coarse, fine, forward, inverse, shards):
    _, rows, channels = cur.shape
    own = channels // coarse.shape[1]
    shard = pl.BlockSpec((2, shards) + coarse.shape[2:], lambda i: (0, i, 0, 0))
    width = own * shards
    block = pl.BlockSpec((1, rows, width), lambda i: (0, 0, i))
    return pl.pallas_call(
        conv_kernel,
        grid=(channels // width,),
        in_specs=[
            block,
            block,
            block,
            shard,
            shard,
            pl.BlockSpec(forward.shape, lambda i: (0, 0)),
            pl.BlockSpec(inverse.shape, lambda i: (0, 0)),
        ],
        out_specs=block,
        out_shape=jax.ShapeDtypeStruct(cur.shape, jnp.bfloat16),
        name="filtered_gate",
    )(prev, cur, query, coarse, fine, forward, inverse)


def per_device(query_proj, key_proj, value_proj, filters):
    f32 = jnp.float32
    peers = lax.axis_size("fsdp")
    own, taps = filters.shape
    halves = (filters * SCALE).astype(WIRE).reshape(1, 2, own // 2, taps)
    send = jnp.broadcast_to(halves, (peers // 2, 2, own // 2, taps)).reshape(peers, own // 2, taps)
    got = lax.all_to_all(send, "fsdp", 0, 0, tiled=True)
    pairs = [[2 * i, 2 * i + 1] for i in range(peers // 2)]
    both = lax.all_to_all(
        jnp.broadcast_to(got[None], (2,) + got.shape), "fsdp", 0, 0, axis_index_groups=pairs, tiled=True
    )
    mixed = (key_proj.astype(f32) * value_proj.astype(f32)).astype(jnp.bfloat16)
    steps = lax.axis_size("seq")
    earlier = lax.ppermute(mixed, "seq", [(i, i + 1) for i in range(steps - 1)])
    forward, inverse = transforms(taps)
    both = both.reshape(2, peers, own // 2, taps).astype(f32)
    coarse = both.astype(jnp.bfloat16)
    fine = (both - coarse.astype(f32)).astype(jnp.bfloat16)
    return filtered_gate(earlier, mixed, query_proj, coarse, fine, forward, inverse, 16)


def solution(mesh):
    rows = P("fsdp", "seq", None)
    return jax.shard_map(
        per_device,
        mesh=mesh,
        in_specs=(rows, rows, rows, P("fsdp", None)),
        out_specs=rows,
        check_vma=False,
    )
```

time: 177 us -> 65.8 us (0.37)
  waiting for transfers between devices: 123 us -> 19.5 us
  starting transfers between devices: 3.98 us -> 26 us
  matrix products: 18.1 us -> 0 us
  between operations: 13.4 us -> 0.05 us
  local copies, waits for them, and re-layouts: 14.5 us -> 1.81 us
  Pallas kernels: 0 us -> 7.61 us
  blocking collectives: 0 us -> 6.29 us
    all_gather x1 -> x0, waiting for transfers between devices: 113 us -> none  [per_device(): lax.all_gather(filters, 'fsdp', axis=0, tiled=True)]
    all_to_all x0 -> x1, starting transfers between devices: none -> 22.8 us  [per_device(): got = lax.all_to_all(send, 'fsdp', 0, 0, tiled=True)]
    all_to_all x0 -> x1, waiting for transfers between devices: none -> 19.5 us  [per_device(): got = lax.all_to_all(send, 'fsdp', 0, 0, tiled=True)]
    conv_general_dilated x1 -> x0, matrix products: 18.1 us -> none  [depthwise(): lax.conv_general_dilated(padded, kernel, (1,), 'VALID', dimension_numbers...]
    rev x1 -> x0, local copies, waits for them, and re-layouts: 11.2 us -> none  [depthwise(): kernel = jnp.transpose(taps[:, ::-1])[:, None, :]]
    ppermute x1, waiting for transfers between devices: 9.28 us -> 0.01 us  [per_device(): earlier = lax.ppermute(mixed, 'seq', [(i, i + 1) for i in range(steps - 1)])]
    pallas_call x0 -> x1, Pallas kernels: none -> 7.61 us  [filtered_gate(): pl.pallas_call(conv_kernel, grid=(channels // width,), in_specs=[block, b...]
    all_to_all x0 -> x1, blocking collectives: none -> 6.29 us  [per_device(): lax.all_to_all(jnp.broadcast_to(got[None], (2,) + got.shape), 'fsdp', 0,...]
  transfers between devices with their start and end apart: 2 -> 2, of which waited for: 2 -> 1; matrix products, arithmetic and copies ran while one was open for 1% -> 5% of each run, Pallas kernels for 0% -> 0%
where the time goes in v1:
time: 65.8 us; the launch traced here: 65.4 us
  starting transfers between devices  26 us (40%)
  waiting for transfers between devices  19.5 us (30%)
  Pallas kernels  7.61 us (12%)
  blocking collectives  6.29 us (10%)
  other arithmetic  4.19 us (6%)
  local copies, waits for them, and re-layouts  1.81 us (3%)
    all_to_all x1, starting transfers between devices, per_device(): got = lax.all_to_all(send, 'fsdp', 0, 0, tiled=True)  22.8 us
    all_to_all x1, waiting for transfers between devices, per_device(): got = lax.all_to_all(send, 'fsdp', 0, 0, tiled=True)  19.5 us
    pallas_call x1, Pallas kernels, filtered_gate(): pl.pallas_call(conv_kernel, grid=(channels // width,), in_specs=[block, b...  7.61 us
    all_to_all x1, blocking collectives, per_device(): lax.all_to_all(jnp.broadcast_to(got[None], (2,) + got.shape), 'fsdp', 0,...  6.29 us
    ppermute x1, starting transfers between devices, per_device(): earlier = lax.ppermute(mixed, 'seq', [(i, i + 1) for i in range(steps - 1)])  3.16 us
    convert_element_type x1, other arithmetic, per_device(): mixed = (key_proj.astype(f32) * value_proj.astype(f32)).astype(jnp.bfloat16)  1.32 us
  transfers between devices with their start and end apart: 2, of which 1 were waited for; matrix products, arithmetic and copies ran while one was open for 5% of the time, Pallas kernels for 0%

profile of v1, /device:TPU:1, one launch (start us, length us, event | category | flops | bytes accessed | tf_op | source)
XLA Modules:
  0.0 65.4 jit_solution(10920328849004984788)
XLA Ops:
  0.0 0.0 copy-start.2
  0.0 0.8 %multiply_convert_fusion.1 = f16[32,128]{1,0:T(8,128)(2,1)S(1)} fusion(f32[32,128]{1,0:T(8,128)} %param.9), kind=kLoop, calls=%fused_computation.4 | loop fusion | flops 8192 | bytes 24576 | tf_op jit(solution)/shard_map/convert_element_type | solution.py:87
  0.8 0.8 %broadcast_in_dim.14 = f16[48,2,16,128]{3,2,1,0:T(8,128)(2,1)} broadcast(f16[2,16,128]{2,1,0:T(8,128)(2,1)S(1)} %bitcast.2), dimensions={1,2,3} | broadcast | bytes 401408 | tf_op jit(solution)/shard_map/broadcast_in_dim | solution.py:88
  1.6 22.8 %all-to-all-start = ((f16[96,16,128]{2,1,0:T(8,128)(2,1)}), f16[96,16,128]{2,1,0:T(8,128)(2,1)S(1)}, u32[]{:S(2)}, u32[]{:S(2)}) async-start(f16[96,16,128]{2,1,0:T(8,128)(2,1)} %bitcast.1), calls=%async_computation | async-start | bytes 786432 | tf_op jit(solution)/shard_map/all_to_all | solution.py:89
  24.4 0.0 copy-done.2
  24.4 1.3 %multiply_convert_fusion.cur_ref = bf16[1,128,3072]{2,1,0:T(8,128)(2,1)S(1)} fusion(bf16[1,128,3072]{2,1,0:T(8,128)(2,1)S(1)} %copy-done.2, bf16[1,128,3072]{2,1,0:T(8,128)(2,1)} %param.7), kind=kLoop, calls=%fused_computation.3 | loop fusion | flops 1572864 | bytes 2359296 | tf_op jit(solution)/shard_map/convert_element_type | solution.py:94
  25.8 0.0 copy-start
  25.8 3.2 %collective-permute-start = (bf16[1,128,3072]{2,1,0:T(8,128)(2,1)S(1)}, bf16[1,128,3072]{2,1,0:T(8,128)(2,1)S(1)}, u32[]{:S(2)}, u32[]{:S(2)}) collective-permute-start(bf16[1,128,3072]{2,1,0:T(8,128)(2,1)S(1)} %multiply_convert_fusion.cur_ref), channel_id=1, source_target_pairs={{0,1},{1,2},{2,3},{3,4},{4,5},{5,6},{6,7},{8,9},{9,10},{10,11},{11... | collective-permute-start | bytes 2359304 | tf_op jit(solution)/shard_map/ppermute | solution.py:96
  28.9 19.5 %all-to-all-done = f16[96,16,128]{2,1,0:T(8,128)(2,1)S(1)} async-done(((f16[96,16,128]{2,1,0:T(8,128)(2,1)}), f16[96,16,128]{2,1,0:T(8,128)(2,1)S(1)}, u32[]{:S(2)}, u32[]{:S(2)}) %all-to-all-start) | async-done | bytes 393248 | tf_op jit(solution)/shard_map/all_to_all | solution.py:89
  48.4 0.1 broadcast_in_dim.15
  48.5 6.3 %all_to_all.10 = f16[2,96,16,128]{3,2,1,0:T(8,128)(2,1)S(1)} all-to-all(f16[2,96,16,128]{3,2,1,0:T(8,128)(2,1)S(1)} %broadcast_in_dim.15), channel_id=1, replica_groups={{0,8},{16,24},{32,40},{48,56},{64,72},{80,88},{96,104},{112,120},{128,1..., dimensions={0} | all-to-all | bytes 1572864 | tf_op jit(solution)/shard_map/all_to_all | solution.py:91
  54.8 0.0 copy-done
  54.8 1.0 %fusion.wl_ref = bf16[2,96,16,128]{3,2,1,0:T(8,128)(2,1)} fusion(f16[2,96,16,128]{3,2,1,0:T(8,128)(2,1)S(1)} %all_to_all.10), kind=kLoop, calls=%fused_computation.2 | loop fusion | flops 1966080 | bytes 1572864 | tf_op jit(solution)/shard_map/convert_element_type | solution.py:100
  55.8 1.0 %convert_convert_fusion.wh_ref = bf16[2,96,16,128]{3,2,1,0:T(8,128)(2,1)} fusion(f16[2,96,16,128]{3,2,1,0:T(8,128)(2,1)S(1)} %all_to_all.10), kind=kLoop, calls=%fused_computation.1 | loop fusion | flops 786432 | bytes 1572864 | tf_op jit(solution)/shard_map/convert_element_type | solution.py:99
  56.9 0.0 collective-permute-done.prev_ref
  56.9 0.0 copy-start.1
  56.9 0.9 %copy-done.1 = bf16[1,128,3072]{2,1,0:T(8,128)(2,1)} copy-done((bf16[1,128,3072]{2,1,0:T(8,128)(2,1)}, bf16[1,128,3072]{2,1,0:T(8,128)(2,1)S(1)}, u32[]{:S(2)}) %copy-start.1) | copy-done | bytes 786456
  57.8 7.6 %filtered_gate.1 = bf16[1,128,3072]{2,1,0:T(8,128)(2,1)} custom-call(bf16[1,128,3072]{2,1,0:T(8,128)(2,1)} %copy-done.1, bf16[1,128,3072]{2,1,0:T(8,128)(2,1)} %copy-done, bf16[1,128,3072]{2,1,0:T(8,128)(2,1)} %query_ref.1, bf16[2,96,16,128]{3,2,1,0:T(8,128)(2,1)} %convert_convert_fusion.wh_ref, bf16[2,96,16,128]{3,2,1,0:T(8,128)(2,1)} %fusion.wl_ref, ...), custom_call_target="tpu_custom_call" | custom-call | tf_op jit(solution)/shard_map/filtered_gate/pallas_call | solution.py:65
Async XLA Ops:
  0.0 24.4 %copy-start.2 = (bf16[1,128,3072]{2,1,0:T(8,128)(2,1)S(1)}, bf16[1,128,3072]{2,1,0:T(8,128)(2,1)}, u32[]{:S(2)}) copy-start(bf16[1,128,3072]{2,1,0:T(8,128)(2,1)} %param.8) | copy-start | bytes 2359300
  1.6 46.8 %all-to-all-start = ((f16[96,16,128]{2,1,0:T(8,128)(2,1)}), f16[96,16,128]{2,1,0:T(8,128)(2,1)S(1)}, u32[]{:S(2)}, u32[]{:S(2)}) async-start(f16[96,16,128]{2,1,0:T(8,128)(2,1)} %bitcast.1), calls=%async_computation | async-start | bytes 786432 | tf_op jit(solution)/shard_map/all_to_all | solution.py:89
  25.8 29.0 %copy-start = (bf16[1,128,3072]{2,1,0:T(8,128)(2,1)}, bf16[1,128,3072]{2,1,0:T(8,128)(2,1)S(1)}, u32[]{:S(2)}) copy-start(bf16[1,128,3072]{2,1,0:T(8,128)(2,1)S(1)} %multiply_convert_fusion.cur_ref) | copy-start | bytes 2359300
  25.8 31.1 %collective-permute-start = (bf16[1,128,3072]{2,1,0:T(8,128)(2,1)S(1)}, bf16[1,128,3072]{2,1,0:T(8,128)(2,1)S(1)}, u32[]{:S(2)}, u32[]{:S(2)}) collective-permute-start(bf16[1,128,3072]{2,1,0:T(8,128)(2,1)S(1)} %multiply_convert_fusion.cur_ref), channel_id=1, source_target_pairs={{0,1},{1,2},{2,3},{3,4},{4,5},{5,6},{6,7},{8,9},{9,10},{10,11},{11... | collective-permute-start | bytes 2359304 | tf_op jit(solution)/shard_map/ppermute | solution.py:96
  56.9 0.9 %copy-start.1 = (bf16[1,128,3072]{2,1,0:T(8,128)(2,1)}, bf16[1,128,3072]{2,1,0:T(8,128)(2,1)S(1)}, u32[]{:S(2)}) copy-start(bf16[1,128,3072]{2,1,0:T(8,128)(2,1)S(1)} %collective-permute-done.prev_ref) | copy-start | bytes 2359300

commit v2 on v1

v2 whole, which is shorter than its diff:
```python
import functools

import jax
import jax.numpy as jnp
import numpy as np
from jax import lax
from jax.experimental import pallas as pl
from jax.sharding import PartitionSpec as P

WIRE = jnp.float16
SCALE = 4096.0


def split(x):
    x = np.asarray(x, np.float32)
    hi = x.astype(jnp.bfloat16)
    return hi, (x - hi.astype(np.float32)).astype(jnp.bfloat16)


def transforms(taps):
    n = 2 * taps
    angle = 2 * np.pi * np.outer(np.arange(taps) + 0.5, np.arange(n)) / n
    forward = np.concatenate([np.cos(angle), -np.sin(angle)])
    inverse = np.concatenate([np.cos(angle), -np.sin(angle)]).T[taps:] / taps
    fh, fl = split(forward)
    gh, gl = split(inverse / SCALE)
    return np.concatenate([fh, fl]), np.concatenate([gh, gl])


def conv_kernel(prev_ref, cur_ref, query_ref, w_ref, f_ref, g_ref, out_ref):
    f32 = jnp.float32
    half, taps = f_ref.shape[0] // 2, cur_ref.shape[1]
    dot = functools.partial(jnp.dot, preferred_element_type=f32)
    f = f_ref[...]
    window = jnp.concatenate([prev_ref[0], cur_ref[0]], axis=0)
    x = dot(f, window)
    x = x[:half] + x[half:]
    w = jnp.concatenate([w_ref[i] for i in range(w_ref.shape[0])], axis=1)
    w = w.reshape(-1, taps)
    wh = w.astype(jnp.bfloat16)
    wl = (w - wh.astype(f32)).astype(jnp.bfloat16)
    nt = functools.partial(
        lax.dot_general, dimension_numbers=(((1,), (1,)), ((), ())), preferred_element_type=f32
    )
    h = nt(f[:, :taps], wh)
    h = h[:half] + h[half:] + nt(f[:half, :taps], wl)
    xr, xi, hr, hi = x[:taps], x[taps:], h[:taps], h[taps:]
    p = jnp.concatenate([xr * hr - xi * hi, xr * hi + xi * hr], axis=0)
    ph = p.astype(jnp.bfloat16)
    plo = (p - ph.astype(f32)).astype(jnp.bfloat16)
    g = g_ref[...]
    y = dot(g, ph)
    y = y[:taps] + y[taps:] + dot(g[:taps], plo)
    out_ref[0] = (query_ref[0].astype(f32) * y).astype(out_ref.dtype)


def filtered_gate(prev, cur, query, taps, forward, inverse, shards):
    _, rows, channels = cur.shape
    own = channels // taps.shape[1]
    width = own * shards
    block = pl.BlockSpec((1, rows, width), lambda i: (0, 0, i))
    return pl.pallas_call(
        conv_kernel,
        grid=(channels // width,),
        in_specs=[
            block,
            block,
            block,
            pl.BlockSpec(taps.shape[:1] + (shards,) + taps.shape[2:], lambda i: (0, i, 0, 0)),
            pl.BlockSpec(forward.shape, lambda i: (0, 0)),
            pl.BlockSpec(inverse.shape, lambda i: (0, 0)),
        ],
        out_specs=block,
        out_shape=jax.ShapeDtypeStruct(cur.shape, jnp.bfloat16),
        name="filtered_gate",
    )(prev, cur, query, taps, forward, inverse)


def per_device(query_proj, key_proj, value_proj, filters):
    f32 = jnp.float32
    peers, steps = lax.axis_size("fsdp"), lax.axis_size("seq")
    own, taps = filters.shape
    part = own // steps
    mine = lax.dynamic_slice_in_dim(filters, lax.axis_index("seq") * part, part, 0)
    mine = (mine * SCALE).astype(WIRE)
    mine = jnp.broadcast_to(mine, (peers, part, taps))
    got = lax.all_to_all(mine, "fsdp", 0, 0, tiled=True)
    got = jnp.broadcast_to(got, (steps,) + got.shape)
    every = lax.all_to_all(got, "seq", 0, 0, tiled=True)
    mixed = (key_proj.astype(f32) * value_proj.astype(f32)).astype(jnp.bfloat16)
    earlier = lax.ppermute(mixed, "seq", [(i, i + 1) for i in range(steps - 1)])
    forward, inverse = transforms(taps)
    every = every.reshape(steps, peers, part, taps).astype(f32)
    return filtered_gate(earlier, mixed, query_proj, every, forward, inverse, 16)


def solution(mesh):
    rows = P("fsdp", "seq", None)
    return jax.shard_map(
        per_device,
        mesh=mesh,
        in_specs=(rows, rows, rows, P("fsdp", None)),
        out_specs=rows,
        check_vma=False,
    )
```

time: 65.8 us -> 81.7 us (1.24)
  the two profiles are of different devices: /device:TPU:1 before, /device:TPU:8 now
where the time goes in v2:
time: 81.7 us; the launch traced here: 81.3 us
  blocking collectives  37.2 us (46%)
  waiting for transfers between devices  22.9 us (28%)
  starting transfers between devices  9.13 us (11%)
  Pallas kernels  7.6 us (9%)
  other arithmetic  2.43 us (3%)
  local copies, waits for them, and re-layouts  2.02 us (2%)
    all_to_all x1, blocking collectives, per_device(): got = lax.all_to_all(mine, 'fsdp', 0, 0, tiled=True)  37.2 us
    ppermute x1, waiting for transfers between devices, per_device(): earlier = lax.ppermute(mixed, 'seq', [(i, i + 1) for i in range(steps - 1)])  13.7 us
    all_to_all x1, waiting for transfers between devices, per_device(): every = lax.all_to_all(got, 'seq', 0, 0, tiled=True)  9.17 us
    pallas_call x1, Pallas kernels, filtered_gate(): pl.pallas_call(conv_kernel, grid=(channels // width,), in_specs=[block, b...  7.6 us
    all_to_all x1, starting transfers between devices, per_device(): every = lax.all_to_all(got, 'seq', 0, 0, tiled=True)  5.76 us
    ppermute x1, starting transfers between devices, per_device(): earlier = lax.ppermute(mixed, 'seq', [(i, i + 1) for i in range(steps - 1)])  3.37 us
  transfers between devices with their start and end apart: 2, of which 2 were waited for; matrix products, arithmetic and copies ran while one was open for 2% of the time, Pallas kernels for 0%

profile of v2, /device:TPU:8, one launch (start us, length us, event | category | flops | bytes accessed | tf_op | source)
XLA Modules:
  0.0 81.3 jit_solution(1784750817231279994)
XLA Ops:
  0.0 0.0 copy-start.2
  0.0 0.0 copy-start.3
  0.0 0.8 %multiply_convert_fusion.1 = f16[4,128]{1,0:T(4,128)(2,1)S(1)} fusion(f32[32,128]{1,0:T(8,128)} %param.9, s32[]{:T(128)S(6)} %select_n.3), kind=kLoop, calls=%fused_computation.1 | loop fusion | flops 1024 | bytes 3076 | tf_op jit(solution)/shard_map/convert_element_type | solution.py:85
  0.9 37.2 %all_to_all.10 = f16[96,4,128]{2,1,0:T(4,128)(2,1)S(1)} all-to-all(f16[96,4,128]{2,1,0:T(4,128)(2,1)S(1)} %broadcast_in_dim.6), channel_id=1, replica_groups=mesh['fsdp'=96,'seq'=8] {'fsdp'}, dimensions={0} | all-to-all | bytes 196608 | tf_op jit(solution)/shard_map/all_to_all | solution.py:87
  38.1 1.1 %broadcast_in_dim.7 = f16[8,96,4,128]{3,2,1,0:T(4,128)(2,1)} broadcast(f16[96,4,128]{2,1,0:T(4,128)(2,1)S(1)} %all_to_all.10), dimensions={1,2,3} | broadcast | bytes 884736 | tf_op jit(solution)/shard_map/broadcast_in_dim | solution.py:88
  39.2 5.8 %all-to-all-start.1 = ((f16[8,96,4,128]{3,2,1,0:T(4,128)(2,1)}), f16[8,96,4,128]{3,2,1,0:T(4,128)(2,1)S(1)}, u32[]{:S(2)}, u32[]{:S(2)}) async-start(f16[8,96,4,128]{3,2,1,0:T(4,128)(2,1)} %broadcast_in_dim.7), calls=%async_computation.1 | async-start | bytes 1572864 | tf_op jit(solution)/shard_map/all_to_all | solution.py:89
  44.9 0.0 copy-done.2
  44.9 0.0 copy-done.3
  44.9 0.2 multiply_convert_fusion.cur_ref
  45.1 0.0 copy-start
  45.1 3.4 %collective-permute-start = (bf16[1,128,3072]{2,1,0:T(8,128)(2,1)S(1)}, bf16[1,128,3072]{2,1,0:T(8,128)(2,1)S(1)}, u32[]{:S(2)}, u32[]{:S(2)}) collective-permute-start(bf16[1,128,3072]{2,1,0:T(8,128)(2,1)S(1)} %multiply_convert_fusion.cur_ref), channel_id=1, source_target_pairs={{0,1},{1,2},{2,3},{3,4},{4,5},{5,6},{6,7},{8,9},{9,10},{10,11},{11... | collective-permute-start | bytes 2359304 | tf_op jit(solution)/shard_map/ppermute | solution.py:91
  48.5 9.2 %all-to-all-done.1 = f16[8,96,4,128]{3,2,1,0:T(4,128)(2,1)S(1)} async-done(((f16[8,96,4,128]{3,2,1,0:T(4,128)(2,1)}), f16[8,96,4,128]{3,2,1,0:T(4,128)(2,1)S(1)}, u32[]{:S(2)}, u32[]{:S(2)}) %all-to-all-start.1) | async-done | bytes 786464 | tf_op jit(solution)/shard_map/all_to_all | solution.py:89
  57.7 1.4 %convert_element_type.19.w_ref = f32[8,96,4,128]{3,2,1,0:T(4,128)} convert(f16[8,96,4,128]{3,2,1,0:T(4,128)(2,1)S(1)} %all-to-all-done.1) | non-fusion elementwise | flops 393216 | bytes 2359296 | tf_op jit(solution)/shard_map/convert_element_type | solution.py:93
  59.1 13.7 %collective-permute-done.prev_ref = bf16[1,128,3072]{2,1,0:T(8,128)(2,1)S(1)} collective-permute-done((bf16[1,128,3072]{2,1,0:T(8,128)(2,1)S(1)}, bf16[1,128,3072]{2,1,0:T(8,128)(2,1)S(1)}, u32[]{:S(2)}, u32[]{:S(2)}) %collective-permute-start) | collective-permute-done | bytes 786464 | tf_op jit(solution)/shard_map/ppermute | solution.py:91
  72.8 0.0 copy-done
  72.8 0.0 copy-start.1
  72.8 0.9 %copy-done.1 = bf16[1,128,3072]{2,1,0:T(8,128)(2,1)} copy-done((bf16[1,128,3072]{2,1,0:T(8,128)(2,1)}, bf16[1,128,3072]{2,1,0:T(8,128)(2,1)S(1)}, u32[]{:S(2)}) %copy-start.1) | copy-done | bytes 786456
  73.7 7.6 %filtered_gate.1 = bf16[1,128,3072]{2,1,0:T(8,128)(2,1)} custom-call(bf16[1,128,3072]{2,1,0:T(8,128)(2,1)} %copy-done.1, bf16[1,128,3072]{2,1,0:T(8,128)(2,1)} %copy-done, bf16[1,128,3072]{2,1,0:T(8,128)(2,1)} %query_ref.1, f32[8,96,4,128]{3,2,1,0:T(4,128)} %convert_element_type.19.w_ref, bf16[512,256]{1,0:T(8,128)(2,1)} %constant.16.clone.f_ref, ...), custom_call_target="tpu_custom_call" | custom-call | tf_op jit(solution)/shard_map/filtered_gate/pallas_call | solution.py:62
  (1 shorter events, 0.0 us)
Async XLA Ops:
  0.0 44.9 %copy-start.2 = (bf16[1,128,3072]{2,1,0:T(8,128)(2,1)S(1)}, bf16[1,128,3072]{2,1,0:T(8,128)(2,1)}, u32[]{:S(2)}) copy-start(bf16[1,128,3072]{2,1,0:T(8,128)(2,1)} %param.8) | copy-start | bytes 2359300
  0.0 44.9 %copy-start.3 = (bf16[1,128,3072]{2,1,0:T(8,128)(2,1)S(1)}, bf16[1,128,3072]{2,1,0:T(8,128)(2,1)}, u32[]{:S(2)}) copy-start(bf16[1,128,3072]{2,1,0:T(8,128)(2,1)} %param.7) | copy-start | bytes 2359300
  39.2 18.5 %all-to-all-start.1 = ((f16[8,96,4,128]{3,2,1,0:T(4,128)(2,1)}), f16[8,96,4,128]{3,2,1,0:T(4,128)(2,1)S(1)}, u32[]{:S(2)}, u32[]{:S(2)}) async-start(f16[8,96,4,128]{3,2,1,0:T(4,128)(2,1)} %broadcast_in_dim.7), calls=%async_computation.1 | async-start | bytes 1572864 | tf_op jit(solution)/shard_map/all_to_all | solution.py:89
  45.1 27.7 %copy-start = (bf16[1,128,3072]{2,1,0:T(8,128)(2,1)}, bf16[1,128,3072]{2,1,0:T(8,128)(2,1)S(1)}, u32[]{:S(2)}) copy-start(bf16[1,128,3072]{2,1,0:T(8,128)(2,1)S(1)} %multiply_convert_fusion.cur_ref) | copy-start | bytes 2359300
  45.1 27.7 %collective-permute-start = (bf16[1,128,3072]{2,1,0:T(8,128)(2,1)S(1)}, bf16[1,128,3072]{2,1,0:T(8,128)(2,1)S(1)}, u32[]{:S(2)}, u32[]{:S(2)}) collective-permute-start(bf16[1,128,3072]{2,1,0:T(8,128)(2,1)S(1)} %multiply_convert_fusion.cur_ref), channel_id=1, source_target_pairs={{0,1},{1,2},{2,3},{3,4},{4,5},{5,6},{6,7},{8,9},{9,10},{10,11},{11... | collective-permute-start | bytes 2359304 | tf_op jit(solution)/shard_map/ppermute | solution.py:91
  72.8 0.9 %copy-start.1 = (bf16[1,128,3072]{2,1,0:T(8,128)(2,1)}, bf16[1,128,3072]{2,1,0:T(8,128)(2,1)S(1)}, u32[]{:S(2)}) copy-start(bf16[1,128,3072]{2,1,0:T(8,128)(2,1)S(1)} %collective-permute-done.prev_ref) | copy-start | bytes 2359300

commit v3 on v2

v3 whole, which is shorter than its diff:
```python
import functools

import jax
import jax.numpy as jnp
import numpy as np
from jax import lax
from jax.experimental import pallas as pl
from jax.experimental.pallas import tpu as pltpu
from jax.sharding import PartitionSpec as P

WIRE = jnp.float16
SCALE = 4096.0

dot = functools.partial(jnp.dot, preferred_element_type=jnp.float32)
dot_rows = functools.partial(
    lax.dot_general, dimension_numbers=(((1,), (1,)), ((), ())), preferred_element_type=jnp.float32
)


def split(x):
    x = np.asarray(x, np.float32)
    hi = x.astype(jnp.bfloat16)
    return hi, (x - hi.astype(np.float32)).astype(jnp.bfloat16)


def transforms(taps):
    n = 2 * taps
    angle = 2 * np.pi * np.outer(np.arange(taps) + 0.5, np.arange(n)) / n
    forward = np.concatenate([np.cos(angle), -np.sin(angle)])
    fh, fl = split(forward)
    gh, gl = split(forward.T[taps:] / (taps * SCALE))
    head, tail = fh[:, :taps], fl[:, :taps]
    return (
        np.concatenate([fh, fl], axis=1),
        np.concatenate([head, head, tail], axis=1),
        np.concatenate([gh, gh, gl], axis=1),
    )


def spectrum_kernel(prev_ref, cur_ref, f_ref, x_ref):
    window = jnp.concatenate([prev_ref[0], cur_ref[0]], axis=0)
    x_ref[...] = dot(f_ref[...], jnp.concatenate([window, window], axis=0))


def gate_kernel(odd_ref, x_ref, mine_ref, other_ref, query_ref, f_ref, g_ref, out_ref):
    f32, bf16 = jnp.float32, jnp.bfloat16
    taps = mine_ref.shape[-1]
    odd = odd_ref[0] == 1
    mine, other = mine_ref[...], other_ref[...]
    w = jnp.concatenate([jnp.where(odd, other, mine), jnp.where(odd, mine, other)], axis=1)
    w = w.reshape(-1, taps)
    wh = w.astype(bf16)
    wl = (w - wh.astype(f32)).astype(bf16)
    h = dot_rows(f_ref[...], jnp.concatenate([wh, wl, wh], axis=1))
    xr, xi, hr, hi = x_ref[:taps], x_ref[taps:], h[:taps], h[taps:]
    p = jnp.concatenate([xr * hr - xi * hi, xr * hi + xi * hr], axis=0)
    ph = p.astype(bf16)
    low = (p - ph.astype(f32)).astype(bf16)
    y = dot(g_ref[...], jnp.concatenate([ph, low, ph], axis=0))
    out_ref[0] = (query_ref[0].astype(f32) * y).astype(out_ref.dtype)


VMEM = pl.BlockSpec(memory_space=pltpu.VMEM)
PARAMS = pltpu.CompilerParams(vmem_limit_bytes=24 << 20)


def spectrum(prev, cur, forward):
    return pl.pallas_call(
        spectrum_kernel,
        in_specs=[VMEM] * 3,
        out_specs=VMEM,
        out_shape=jax.ShapeDtypeStruct((forward.shape[0], cur.shape[2]), jnp.float32),
        compiler_params=PARAMS,
        name="spectrum",
    )(prev, cur, forward)


def gate(odd, x, mine, other, query, forward, inverse):
    return pl.pallas_call(
        gate_kernel,
        in_specs=[pl.BlockSpec(memory_space=pltpu.SMEM)] + [VMEM] * 6,
        out_specs=VMEM,
        out_shape=jax.ShapeDtypeStruct(query.shape, jnp.bfloat16),
        compiler_params=PARAMS,
        name="gate",
    )(odd, x, mine, other, query, forward, inverse)


def per_device(query_proj, key_proj, value_proj, filters):
    f32 = jnp.float32
    peers, steps = lax.axis_size("fsdp"), lax.axis_size("seq")
    own, taps = filters.shape
    window_dft, taps_dft, inverse = transforms(taps)
    mixed = (key_proj.astype(f32) * value_proj.astype(f32)).astype(jnp.bfloat16)
    earlier = lax.ppermute(mixed, "seq", [(i, i + 1) for i in range(steps - 1)])
    halves = (filters * SCALE).astype(WIRE).reshape(1, 2, own // 2, taps)
    send = jnp.broadcast_to(halves, (peers // 2, 2, own // 2, taps))
    mine = lax.all_to_all(send.reshape(peers, own // 2, taps), "fsdp", 0, 0, tiled=True)
    x = spectrum(earlier, mixed, window_dft)
    other = lax.ppermute(mine, "fsdp", [(i, i ^ 1) for i in range(peers)])
    mine = mine.astype(f32)
    odd = (lax.axis_index("fsdp") % 2).astype(jnp.int32).reshape(1)
    return gate(odd, x, mine, other.astype(f32), query_proj, taps_dft, inverse)


def solution(mesh):
    rows = P("fsdp", "seq", None)
    return jax.shard_map(
        per_device,
        mesh=mesh,
        in_specs=(rows, rows, rows, P("fsdp", None)),
        out_specs=rows,
        check_vma=False,
    )
```

time: 81.7 us -> 61 us (0.75)
  the two profiles are of different devices: /device:TPU:8 before, /device:TPU:56 now
where the time goes in v3:
time: 61 us; the launch traced here: 60.7 us
  starting transfers between devices  27 us (44%)
  waiting for transfers between devices  25.2 us (41%)
  Pallas kernels  4.28 us (7%)
  other arithmetic  2.23 us (4%)
  local copies, waits for them, and re-layouts  1.87 us (3%)
    all_to_all x1, starting transfers between devices, per_device(): lax.all_to_all(send.reshape(peers, own // 2, taps), 'fsdp', 0, 0, tiled=T...  21.7 us
    all_to_all x1, waiting for transfers between devices, per_device(): lax.all_to_all(send.reshape(peers, own // 2, taps), 'fsdp', 0, 0, tiled=T...  17.4 us
    ppermute x1, waiting for transfers between devices, per_device(): earlier = lax.ppermute(mixed, 'seq', [(i, i + 1) for i in range(steps - 1)])  7.73 us
    ppermute x1, starting transfers between devices, per_device(): earlier = lax.ppermute(mixed, 'seq', [(i, i + 1) for i in range(steps - 1)])  3.4 us
    pallas_call x1, Pallas kernels, gate(): pl.pallas_call(gate_kernel, in_specs=[pl.BlockSpec(memory_space=pltpu.SME...  3.3 us
    ppermute x1, starting transfers between devices, per_device(): other = lax.ppermute(mine, 'fsdp', [(i, i ^ 1) for i in range(peers)])  1.91 us
    convert_element_type x1, other arithmetic, per_device(): mixed = (key_proj.astype(f32) * value_proj.astype(f32)).astype(jnp.bfloat16)  1.32 us
  transfers between devices with their start and end apart: 3, of which 2 were waited for; matrix products, arithmetic and copies ran while one was open for 2% of the time, Pallas kernels for 2%

profile of v3, /device:TPU:56, one launch (start us, length us, event | category | flops | bytes accessed | tf_op | source)
XLA Modules:
  0.0 60.7 jit_solution(5411675174723022570)
XLA Ops:
  0.0 0.0 copy-start.4
  0.0 0.8 %multiply_convert_fusion.1 = f16[32,128]{1,0:T(8,128)(2,1)S(1)} fusion(f32[32,128]{1,0:T(8,128)} %param.10), kind=kLoop, calls=%fused_computation.1 | loop fusion | flops 8192 | bytes 24576 | tf_op jit(solution)/shard_map/convert_element_type | solution.py:96
  0.8 0.8 %broadcast_in_dim.8 = f16[48,2,16,128]{3,2,1,0:T(8,128)(2,1)} broadcast(f16[2,16,128]{2,1,0:T(8,128)(2,1)S(1)} %bitcast.3), dimensions={1,2,3} | broadcast | bytes 401408 | tf_op jit(solution)/shard_map/broadcast_in_dim | solution.py:97
  1.6 0.0 copy-start.1
  1.6 21.7 %all-to-all-start = ((f16[96,16,128]{2,1,0:T(8,128)(2,1)}), f16[96,16,128]{2,1,0:T(8,128)(2,1)S(1)}, u32[]{:S(2)}, u32[]{:S(2)}) async-start(f16[96,16,128]{2,1,0:T(8,128)(2,1)} %bitcast.2), calls=%async_computation | async-start | bytes 786432 | tf_op jit(solution)/shard_map/all_to_all | solution.py:98
  23.3 0.0 copy-done.4
  23.3 1.3 %multiply_convert_fusion.cur_ref = bf16[1,128,3072]{2,1,0:T(8,128)(2,1)S(1)} fusion(bf16[1,128,3072]{2,1,0:T(8,128)(2,1)S(1)} %copy-done.4, bf16[1,128,3072]{2,1,0:T(8,128)(2,1)} %param.8), kind=kLoop, calls=%fused_computation | loop fusion | flops 1572864 | bytes 2359296 | tf_op jit(solution)/shard_map/convert_element_type | solution.py:94
  24.7 3.4 %collective-permute-start = (bf16[1,128,3072]{2,1,0:T(8,128)(2,1)S(1)}, bf16[1,128,3072]{2,1,0:T(8,128)(2,1)S(1)}, u32[]{:S(2)}, u32[]{:S(2)}) collective-permute-start(bf16[1,128,3072]{2,1,0:T(8,128)(2,1)S(1)} %multiply_convert_fusion.cur_ref), channel_id=1, source_target_pairs={{0,1},{1,2},{2,3},{3,4},{4,5},{5,6},{6,7},{8,9},{9,10},{10,11},{11... | collective-permute-start | bytes 2359304 | tf_op jit(solution)/shard_map/ppermute | solution.py:95
  28.1 17.4 %all-to-all-done = f16[96,16,128]{2,1,0:T(8,128)(2,1)S(1)} async-done(((f16[96,16,128]{2,1,0:T(8,128)(2,1)}), f16[96,16,128]{2,1,0:T(8,128)(2,1)S(1)}, u32[]{:S(2)}, u32[]{:S(2)}) %all-to-all-start) | async-done | bytes 393248 | tf_op jit(solution)/shard_map/all_to_all | solution.py:98
  45.5 1.9 %collective-permute-start.1 = (f16[96,16,128]{2,1,0:T(8,128)(2,1)S(1)}, f16[96,16,128]{2,1,0:T(8,128)(2,1)S(1)}, u32[]{:S(2)}, u32[]{:S(2)}) collective-permute-start(f16[96,16,128]{2,1,0:T(8,128)(2,1)S(1)} %all-to-all-done), channel_id=1, source_target_pairs={{0,8},{8,0},{16,24},{24,16},{32,40},{40,32},{48,56},{56,48},{64,72... | collective-permute-start | bytes 1179656 | tf_op jit(solution)/shard_map/ppermute | solution.py:100
  47.4 7.7 %collective-permute-done.prev_ref = bf16[1,128,3072]{2,1,0:T(8,128)(2,1)S(1)} collective-permute-done((bf16[1,128,3072]{2,1,0:T(8,128)(2,1)S(1)}, bf16[1,128,3072]{2,1,0:T(8,128)(2,1)S(1)}, u32[]{:S(2)}, u32[]{:S(2)}) %collective-permute-start) | collective-permute-done | bytes 786464 | tf_op jit(solution)/shard_map/ppermute | solution.py:95
  55.1 0.0 copy-done.1
  55.2 1.0 %spectrum.1.x_ref = f32[256,3072]{1,0:T(8,128)S(1)} custom-call(bf16[1,128,3072]{2,1,0:T(8,128)(2,1)S(1)} %collective-permute-done.prev_ref, bf16[1,128,3072]{2,1,0:T(8,128)(2,1)S(1)} %multiply_convert_fusion.cur_ref, bf16[256,512]{1,0:T(8,128)(2,1)S(1)} %copy-done.1), custom_call_target="tpu_custom_call" | custom-call | tf_op jit(solution)/shard_map/spectrum/pallas_call | solution.py:68
  56.1 0.0 copy-start
  56.1 0.0 copy-start.2
  56.2 0.0 copy-start.3
  56.2 0.1 convert_element_type.22.mine_ref
  56.2 0.0 collective-permute-done.1
  56.2 0.1 convert_element_type.23.other_ref
  56.3 1.0 %copy-done = bf16[1,128,3072]{2,1,0:T(8,128)(2,1)S(1)} copy-done((bf16[1,128,3072]{2,1,0:T(8,128)(2,1)S(1)}, bf16[1,128,3072]{2,1,0:T(8,128)(2,1)}, u32[]{:S(2)}) %copy-start) | copy-done | bytes 786456
  57.3 0.0 copy-done.2
  57.3 0.1 copy-done.3
  57.4 3.3 %gate.1 = bf16[1,128,3072]{2,1,0:T(8,128)(2,1)} custom-call(s32[1]{0:T(128)} %bitcast.odd_ref, f32[256,3072]{1,0:T(8,128)S(1)} %spectrum.1.x_ref, f32[96,16,128]{2,1,0:T(8,128)S(1)} %convert_element_type.22.mine_ref, f32[96,16,128]{2,1,0:T(8,128)S(1)} %convert_element_type.23.other_ref, bf16[1,128,3072]{2,1,0:T(8,128)(2,1)S(1)} %copy-done, ...), custom_call_target="tpu_custom_call" | custom-call | tf_op jit(solution)/shard_map/gate/pallas_call | solution.py:79
Async XLA Ops:
  0.0 23.3 %copy-start.4 = (bf16[1,128,3072]{2,1,0:T(8,128)(2,1)S(1)}, bf16[1,128,3072]{2,1,0:T(8,128)(2,1)}, u32[]{:S(2)}) copy-start(bf16[1,128,3072]{2,1,0:T(8,128)(2,1)} %param.9) | copy-start | bytes 2359300
  1.6 53.5 %copy-start.1 = (bf16[256,512]{1,0:T(8,128)(2,1)S(1)}, bf16[256,512]{1,0:T(8,128)(2,1)}, u32[]{:S(2)}) copy-start(bf16[256,512]{1,0:T(8,128)(2,1)} %constant.26.clone.f_ref) | copy-start | bytes 786436
  1.6 43.9 %all-to-all-start = ((f16[96,16,128]{2,1,0:T(8,128)(2,1)}), f16[96,16,128]{2,1,0:T(8,128)(2,1)S(1)}, u32[]{:S(2)}, u32[]{:S(2)}) async-start(f16[96,16,128]{2,1,0:T(8,128)(2,1)} %bitcast.2), calls=%async_computation | async-start | bytes 786432 | tf_op jit(solution)/shard_map/all_to_all | solution.py:98
  24.7 30.5 %collective-permute-start = (bf16[1,128,3072]{2,1,0:T(8,128)(2,1)S(1)}, bf16[1,128,3072]{2,1,0:T(8,128)(2,1)S(1)}, u32[]{:S(2)}, u32[]{:S(2)}) collective-permute-start(bf16[1,128,3072]{2,1,0:T(8,128)(2,1)S(1)} %multiply_convert_fusion.cur_ref), channel_id=1, source_target_pairs={{0,1},{1,2},{2,3},{3,4},{4,5},{5,6},{6,7},{8,9},{9,10},{10,11},{11... | collective-permute-start | bytes 2359304 | tf_op jit(solution)/shard_map/ppermute | solution.py:95
  45.5 10.7 %collective-permute-start.1 = (f16[96,16,128]{2,1,0:T(8,128)(2,1)S(1)}, f16[96,16,128]{2,1,0:T(8,128)(2,1)S(1)}, u32[]{:S(2)}, u32[]{:S(2)}) collective-permute-start(f16[96,16,128]{2,1,0:T(8,128)(2,1)S(1)} %all-to-all-done), channel_id=1, source_target_pairs={{0,8},{8,0},{16,24},{24,16},{32,40},{40,32},{48,56},{56,48},{64,72... | collective-permute-start | bytes 1179656 | tf_op jit(solution)/shard_map/ppermute | solution.py:100
  56.1 1.1 %copy-start = (bf16[1,128,3072]{2,1,0:T(8,128)(2,1)S(1)}, bf16[1,128,3072]{2,1,0:T(8,128)(2,1)}, u32[]{:S(2)}) copy-start(bf16[1,128,3072]{2,1,0:T(8,128)(2,1)} %query_ref.1) | copy-start | bytes 2359300
  56.1 1.2 %copy-start.2 = (bf16[256,384]{1,0:T(8,128)(2,1)S(1)}, bf16[256,384]{1,0:T(8,128)(2,1)}, u32[]{:S(2)}) copy-start(bf16[256,384]{1,0:T(8,128)(2,1)} %constant.27.clone.f_ref) | copy-start | bytes 589828
  56.2 1.2 %copy-start.3 = (bf16[128,768]{1,0:T(8,128)(2,1)S(1)}, bf16[128,768]{1,0:T(8,128)(2,1)}, u32[]{:S(2)}) copy-start(bf16[128,768]{1,0:T(8,128)(2,1)} %constant.28.clone.g_ref) | copy-start | bytes 589828

commit v4 on v3

v4 whole, which is shorter than its diff:
```python
import functools

import jax
import jax.numpy as jnp
import numpy as np
from jax import lax
from jax.experimental import pallas as pl
from jax.experimental.pallas import tpu as pltpu
from jax.sharding import PartitionSpec as P

WIRE = jnp.float16
SCALE = 4096.0

dot = functools.partial(jnp.dot, preferred_element_type=jnp.float32)
dot_rows = functools.partial(
    lax.dot_general, dimension_numbers=(((1,), (1,)), ((), ())), preferred_element_type=jnp.float32
)


def split(x):
    x = np.asarray(x, np.float32)
    hi = x.astype(jnp.bfloat16)
    return hi, (x - hi.astype(np.float32)).astype(jnp.bfloat16)


def transforms(taps):
    n = 2 * taps
    angle = 2 * np.pi * np.outer(np.arange(taps) + 0.5, np.arange(n)) / n
    forward = np.concatenate([np.cos(angle), -np.sin(angle)])
    fh, fl = split(forward)
    gh, gl = split(forward.T[taps:] / (taps * SCALE))
    head, tail = fh[:, :taps], fl[:, :taps]
    return (
        np.concatenate([fh, fl], axis=1),
        np.block([[head, head], [tail, np.zeros_like(tail)]]),
        np.concatenate([gh, gl], axis=0),
    )


def spectrum_kernel(prev_ref, key_ref, value_ref, f_ref, x_ref):
    f32 = jnp.float32
    mixed = (key_ref[0].astype(f32) * value_ref[0].astype(f32)).astype(jnp.bfloat16)
    window = jnp.concatenate([prev_ref[0], mixed], axis=0)
    x_ref[...] = dot(f_ref[...], jnp.concatenate([window, window], axis=0))


def gate_kernel(x_ref, w_ref, query_ref, f_ref, g_ref, out_ref):
    f32, bf16 = jnp.float32, jnp.bfloat16
    steps, peers, part, taps = w_ref.shape
    w = jnp.concatenate([w_ref[i] for i in range(steps)], axis=1)
    w = w.reshape(steps * peers * part, taps)
    wh = w.astype(bf16)
    wl = (w - wh.astype(f32)).astype(bf16)
    h = dot_rows(f_ref[...], jnp.concatenate([wh, wl], axis=1))
    h = h[: 2 * taps] + h[2 * taps :]
    xr, xi, hr, hi = x_ref[:taps], x_ref[taps:], h[:taps], h[taps:]
    p = jnp.concatenate([xr * hr - xi * hi, xr * hi + xi * hr], axis=0)
    ph = p.astype(bf16)
    low = (p - ph.astype(f32)).astype(bf16)
    y = dot(g_ref[...], ph)
    y = y[:taps] + y[taps:] + dot(g_ref[:taps], low)
    out_ref[0] = (query_ref[0].astype(f32) * y).astype(out_ref.dtype)


VMEM = pl.BlockSpec(memory_space=pltpu.VMEM)
PARAMS = pltpu.CompilerParams(vmem_limit_bytes=24 << 20)


def spectrum(prev, key, value, forward):
    return pl.pallas_call(
        spectrum_kernel,
        in_specs=[VMEM] * 4,
        out_specs=VMEM,
        out_shape=jax.ShapeDtypeStruct((forward.shape[0], key.shape[2]), jnp.float32),
        compiler_params=PARAMS,
        name="spectrum",
    )(prev, key, value, forward)


def gate(x, w, query, forward, inverse):
    return pl.pallas_call(
        gate_kernel,
        in_specs=[VMEM] * 5,
        out_specs=VMEM,
        out_shape=jax.ShapeDtypeStruct(query.shape, jnp.bfloat16),
        compiler_params=PARAMS,
        name="gate",
    )(x, w, query, forward, inverse)


def per_device(query_proj, key_proj, value_proj, filters):
    f32 = jnp.float32
    peers, steps = lax.axis_size("fsdp"), lax.axis_size("seq")
    own, taps = filters.shape
    part = own // steps
    window_dft, taps_dft, inverse = transforms(taps)
    mixed = (key_proj.astype(f32) * value_proj.astype(f32)).astype(jnp.bfloat16)
    earlier = lax.ppermute(mixed, "seq", [(i, i + 1) for i in range(steps - 1)])
    mine = lax.dynamic_slice_in_dim(filters, lax.axis_index("seq") * part, part, 0)
    mine = (mine * SCALE).astype(WIRE)
    mine = jnp.broadcast_to(mine, (peers, part, taps))
    got = lax.all_to_all(mine, "fsdp", 0, 0, tiled=True)
    x = spectrum(earlier, key_proj, value_proj, window_dft)
    got = jnp.broadcast_to(got, (steps,) + got.shape)
    every = lax.all_to_all(got, "seq", 0, 0, tiled=True)
    every = every.reshape(steps, peers, part, taps).astype(f32)
    return gate(x, every, query_proj, taps_dft, inverse)


def solution(mesh):
    rows = P("fsdp", "seq", None)
    return jax.shard_map(
        per_device,
        mesh=mesh,
        in_specs=(rows, rows, rows, P("fsdp", None)),
        out_specs=rows,
        check_vma=False,
    )
```

time: 61 us -> 78.7 us (1.29)
  the two profiles are of different devices: /device:TPU:56 before, /device:TPU:8 now
where the time goes in v4:
time: 78.7 us; the launch traced here: 78.5 us
  blocking collectives  37.2 us (47%)
  waiting for transfers between devices  24.2 us (31%)
  starting transfers between devices  9.39 us (12%)
  Pallas kernels  3.94 us (5%)
  other arithmetic  2.49 us (3%)
  local copies, waits for them, and re-layouts  1.16 us (1%)
    all_to_all x1, blocking collectives, per_device(): got = lax.all_to_all(mine, 'fsdp', 0, 0, tiled=True)  37.2 us
    ppermute x1, waiting for transfers between devices, per_device(): earlier = lax.ppermute(mixed, 'seq', [(i, i + 1) for i in range(steps - 1)])  24.2 us
    all_to_all x1, starting transfers between devices, per_device(): every = lax.all_to_all(got, 'seq', 0, 0, tiled=True)  5.89 us
    ppermute x1, starting transfers between devices, per_device(): earlier = lax.ppermute(mixed, 'seq', [(i, i + 1) for i in range(steps - 1)])  3.5 us
    pallas_call x1, Pallas kernels, gate(): pl.pallas_call(gate_kernel, in_specs=[VMEM] * 5, out_specs=VMEM, out_shap...  2.95 us
  transfers between devices with their start and end apart: 2, of which 1 were waited for; matrix products, arithmetic and copies ran while one was open for 0% of the time, Pallas kernels for 1%

profile of v4, /device:TPU:8, one launch (start us, length us, event | category | flops | bytes accessed | tf_op | source)
XLA Modules:
  0.0 78.5 jit_solution(9708421768101248956)
XLA Ops:
  0.0 0.8 %multiply_convert_fusion.1 = f16[4,128]{1,0:T(4,128)(2,1)S(1)} fusion(f32[32,128]{1,0:T(8,128)} %param.10, s32[]{:T(128)S(6)} %select_n.3), kind=kLoop, calls=%fused_computation.1 | loop fusion | flops 1024 | bytes 3076 | tf_op jit(solution)/shard_map/convert_element_type | solution.py:100
  0.9 37.2 %all_to_all.10 = f16[96,4,128]{2,1,0:T(4,128)(2,1)S(1)} all-to-all(f16[96,4,128]{2,1,0:T(4,128)(2,1)S(1)} %broadcast_in_dim.6), channel_id=1, replica_groups=mesh['fsdp'=96,'seq'=8] {'fsdp'}, dimensions={0} | all-to-all | bytes 196608 | tf_op jit(solution)/shard_map/all_to_all | solution.py:102
  38.1 1.1 %broadcast_in_dim.7 = f16[8,96,4,128]{3,2,1,0:T(4,128)(2,1)} broadcast(f16[96,4,128]{2,1,0:T(4,128)(2,1)S(1)} %all_to_all.10), dimensions={1,2,3} | broadcast | bytes 884736 | tf_op jit(solution)/shard_map/broadcast_in_dim | solution.py:104
  39.2 5.9 %all-to-all-start.1 = ((f16[8,96,4,128]{3,2,1,0:T(4,128)(2,1)}), f16[8,96,4,128]{3,2,1,0:T(4,128)(2,1)}, u32[]{:S(2)}, u32[]{:S(2)}) async-start(f16[8,96,4,128]{3,2,1,0:T(4,128)(2,1)} %broadcast_in_dim.7), calls=%async_computation.1 | async-start | bytes 1572864 | tf_op jit(solution)/shard_map/all_to_all | solution.py:105
  45.0 0.0 copy-done
  45.0 0.0 copy-done.2
  45.1 0.0 copy-start.1
  45.1 0.0 copy-start.3
  45.1 0.2 multiply_convert_fusion
  45.3 3.5 %collective-permute-start = (bf16[1,128,3072]{2,1,0:T(8,128)(2,1)S(1)}, bf16[1,128,3072]{2,1,0:T(8,128)(2,1)S(1)}, u32[]{:S(2)}, u32[]{:S(2)}) collective-permute-start(bf16[1,128,3072]{2,1,0:T(8,128)(2,1)S(1)} %multiply_convert_fusion), channel_id=1, source_target_pairs={{0,1},{1,2},{2,3},{3,4},{4,5},{5,6},{6,7},{8,9},{9,10},{10,11},{11... | collective-permute-start | bytes 2359304 | tf_op jit(solution)/shard_map/ppermute | solution.py:98
  48.8 24.2 %collective-permute-done.prev_ref = bf16[1,128,3072]{2,1,0:T(8,128)(2,1)S(1)} collective-permute-done((bf16[1,128,3072]{2,1,0:T(8,128)(2,1)S(1)}, bf16[1,128,3072]{2,1,0:T(8,128)(2,1)S(1)}, u32[]{:S(2)}, u32[]{:S(2)}) %collective-permute-start) | collective-permute-done | bytes 786464 | tf_op jit(solution)/shard_map/ppermute | solution.py:98
  72.9 0.0 copy-done.6
  72.9 0.0 copy-done.1
  72.9 0.0 copy-done.3
  72.9 1.0 %spectrum.1.x_ref = f32[256,3072]{1,0:T(8,128)S(1)} custom-call(bf16[1,128,3072]{2,1,0:T(8,128)(2,1)S(1)} %collective-permute-done.prev_ref, bf16[1,128,3072]{2,1,0:T(8,128)(2,1)S(1)} %copy-done.3, bf16[1,128,3072]{2,1,0:T(8,128)(2,1)S(1)} %copy-done.1, bf16[256,512]{1,0:T(8,128)(2,1)S(1)} %copy-done.6), custom_call_target="tpu_custom_call" | custom-call | tf_op jit(solution)/shard_map/spectrum/pallas_call | solution.py:70
  73.9 0.0 copy-start.5
  74.0 0.0 copy-start.7
  74.0 0.0 all-to-all-done.1
  74.0 0.0 copy-start.4
  74.0 1.5 %convert_element_type.19.w_ref = f32[8,96,4,128]{3,2,1,0:T(4,128)S(1)} convert(f16[8,96,4,128]{3,2,1,0:T(4,128)(2,1)} %all-to-all-done.1) | non-fusion elementwise | flops 393216 | bytes 2359296 | tf_op jit(solution)/shard_map/convert_element_type | solution.py:106
  75.5 0.0 copy-done.5
  75.5 0.0 copy-done.7
  75.5 0.0 copy-done.4
  75.5 2.9 %gate.1 = bf16[1,128,3072]{2,1,0:T(8,128)(2,1)} custom-call(f32[256,3072]{1,0:T(8,128)S(1)} %spectrum.1.x_ref, f32[8,96,4,128]{3,2,1,0:T(4,128)S(1)} %convert_element_type.19.w_ref, bf16[1,128,3072]{2,1,0:T(8,128)(2,1)S(1)} %copy-done.4, bf16[512,256]{1,0:T(8,128)(2,1)S(1)} %copy-done.5, bf16[256,256]{1,0:T(8,128)(2,1)S(1)} %copy-done.7), custom_call_target="tpu_custom_call" | custom-call | tf_op jit(solution)/shard_map/gate/pallas_call | solution.py:81
  (4 shorter events, 0.0 us)
Async XLA Ops:
  0.0 45.0 %copy-start = (bf16[1,128,3072]{2,1,0:T(8,128)(2,1)S(1)}, bf16[1,128,3072]{2,1,0:T(8,128)(2,1)}, u32[]{:S(2)}) copy-start(bf16[1,128,3072]{2,1,0:T(8,128)(2,1)} %value_ref.1) | copy-start | bytes 2359300
  0.0 45.0 %copy-start.2 = (bf16[1,128,3072]{2,1,0:T(8,128)(2,1)S(1)}, bf16[1,128,3072]{2,1,0:T(8,128)(2,1)}, u32[]{:S(2)}) copy-start(bf16[1,128,3072]{2,1,0:T(8,128)(2,1)} %key_ref.1) | copy-start | bytes 2359300
  39.2 33.8 %copy-start.6 = (bf16[256,512]{1,0:T(8,128)(2,1)S(1)}, bf16[256,512]{1,0:T(8,128)(2,1)}, u32[]{:S(2)}) copy-start(bf16[256,512]{1,0:T(8,128)(2,1)} %constant.18.clone.f_ref) | copy-start | bytes 786436
  39.2 34.8 %all-to-all-start.1 = ((f16[8,96,4,128]{3,2,1,0:T(4,128)(2,1)}), f16[8,96,4,128]{3,2,1,0:T(4,128)(2,1)}, u32[]{:S(2)}, u32[]{:S(2)}) async-start(f16[8,96,4,128]{3,2,1,0:T(4,128)(2,1)} %broadcast_in_dim.7), calls=%async_computation.1 | async-start | bytes 1572864 | tf_op jit(solution)/shard_map/all_to_all | solution.py:105
  45.1 27.9 %copy-start.1 = (bf16[1,128,3072]{2,1,0:T(8,128)(2,1)S(1)}, bf16[1,128,3072]{2,1,0:T(8,128)(2,1)}, u32[]{:S(2)}) copy-start(bf16[1,128,3072]{2,1,0:T(8,128)(2,1)} %value_ref.1) | copy-start | bytes 2359300
  45.1 27.9 %copy-start.3 = (bf16[1,128,3072]{2,1,0:T(8,128)(2,1)S(1)}, bf16[1,128,3072]{2,1,0:T(8,128)(2,1)}, u32[]{:S(2)}) copy-start(bf16[1,128,3072]{2,1,0:T(8,128)(2,1)} %key_ref.1) | copy-start | bytes 2359300
  45.3 27.7 %collective-permute-start = (bf16[1,128,3072]{2,1,0:T(8,128)(2,1)S(1)}, bf16[1,128,3072]{2,1,0:T(8,128)(2,1)S(1)}, u32[]{:S(2)}, u32[]{:S(2)}) collective-permute-start(bf16[1,128,3072]{2,1,0:T(8,128)(2,1)S(1)} %multiply_convert_fusion), channel_id=1, source_target_pairs={{0,1},{1,2},{2,3},{3,4},{4,5},{5,6},{6,7},{8,9},{9,10},{10,11},{11... | collective-permute-start | bytes 2359304 | tf_op jit(solution)/shard_map/ppermute | solution.py:98
  73.9 1.5 %copy-start.5 = (bf16[512,256]{1,0:T(8,128)(2,1)S(1)}, bf16[512,256]{1,0:T(8,128)(2,1)}, u32[]{:S(2)}) copy-start(bf16[512,256]{1,0:T(8,128)(2,1)} %constant.19.clone.f_ref) | copy-start | bytes 786436
  74.0 1.5 %copy-start.7 = (bf16[256,256]{1,0:T(8,128)(2,1)S(1)}, bf16[256,256]{1,0:T(8,128)(2,1)}, u32[]{:S(2)}) copy-start(bf16[256,256]{1,0:T(8,128)(2,1)} %constant.20.clone.g_ref) | copy-start | bytes 393220
  74.0 1.5 %copy-start.4 = (bf16[1,128,3072]{2,1,0:T(8,128)(2,1)S(1)}, bf16[1,128,3072]{2,1,0:T(8,128)(2,1)}, u32[]{:S(2)}) copy-start(bf16[1,128,3072]{2,1,0:T(8,128)(2,1)} %query_ref.1) | copy-start | bytes 2359300

commit v5 on v4

--- a/solution.py
+++ b/solution.py
@@ -44,11 +44,15 @@
     x_ref[...] = dot(f_ref[...], jnp.concatenate([window, window], axis=0))
 
 
-def gate_kernel(x_ref, w_ref, query_ref, f_ref, g_ref, out_ref):
+def gate_kernel(odd_ref, x_ref, mine_ref, other_ref, query_ref, f_ref, g_ref, out_ref):
     f32, bf16 = jnp.float32, jnp.bfloat16
-    steps, peers, part, taps = w_ref.shape
-    w = jnp.concatenate([w_ref[i] for i in range(steps)], axis=1)
-    w = w.reshape(steps * peers * part, taps)
+    taps = mine_ref.shape[-1]
+    odd = odd_ref[0] == 1
+    pieces = []
+    for i in range(mine_ref.shape[0]):
+        mine, other = mine_ref[i], other_ref[i]
+        pieces += [jnp.where(odd, other, mine), jnp.where(odd, mine, other)]
+    w = jnp.concatenate(pieces, axis=1).reshape(-1, taps)
     wh = w.astype(bf16)
     wl = (w - wh.astype(f32)).astype(bf16)
     h = dot_rows(f_ref[...], jnp.concatenate([wh, wl], axis=1))
@@ -77,34 +81,46 @@
     )(prev, key, value, forward)
 
 
-def gate(x, w, query, forward, inverse):
+def gate(odd, x, mine, other, query, forward, inverse):
     return pl.pallas_call(
         gate_kernel,
-        in_specs=[VMEM] * 5,
+        in_specs=[pl.BlockSpec(memory_space=pltpu.SMEM)] + [VMEM] * 6,
         out_specs=VMEM,
         out_shape=jax.ShapeDtypeStruct(query.shape, jnp.bfloat16),
         compiler_params=PARAMS,
         name="gate",
-    )(x, w, query, forward, inverse)
+    )(odd, x, mine, other, query, forward, inverse)
+
+
+NEAR = 4
+
+
+def stage_groups(peers):
+    index = np.arange(peers).reshape(-1, NEAR, 2)
+    far = [index[:, near, core].tolist() for near in range(NEAR) for core in range(2)]
+    near = [index[chunk, :, core].tolist() for chunk in range(index.shape[0]) for core in range(2)]
+    return far, near
+
+
+def exchange(piece, groups):
+    copies = jnp.broadcast_to(piece, (len(groups[0]),) + piece.shape)
+    return lax.all_to_all(copies, "fsdp", 0, 0, axis_index_groups=groups, tiled=True)
 
 
 def per_device(query_proj, key_proj, value_proj, filters):
     f32 = jnp.float32
     peers, steps = lax.axis_size("fsdp"), lax.axis_size("seq")
-    own, taps = filters.shape
-    part = own // steps
-    window_dft, taps_dft, inverse = transforms(taps)
+    window_dft, taps_dft, inverse = transforms(filters.shape[1])
+    far, near = stage_groups(peers)
+    mine = exchange((filters * SCALE).astype(WIRE), far)
     mixed = (key_proj.astype(f32) * value_proj.astype(f32)).astype(jnp.bfloat16)
     earlier = lax.ppermute(mixed, "seq", [(i, i + 1) for i in range(steps - 1)])
-    mine = lax.dynamic_slice_in_dim(filters, lax.axis_index("seq") * part, part, 0)
-    mine = (mine * SCALE).astype(WIRE)
-    mine = jnp.broadcast_to(mine, (peers, part, taps))
-    got = lax.all_to_all(mine, "fsdp", 0, 0, tiled=True)
+    mine = exchange(mine, near)
     x = spectrum(earlier, key_proj, value_proj, window_dft)
-    got = jnp.broadcast_to(got, (steps,) + got.shape)
-    every = lax.all_to_all(got, "seq", 0, 0, tiled=True)
-    every = every.reshape(steps, peers, part, taps).astype(f32)
-    return gate(x, every, query_proj, taps_dft, inverse)
+    other = lax.ppermute(mine, "fsdp", [(i, i ^ 1) for i in range(peers)])
+    mine = mine.astype(f32)
+    odd = (lax.axis_index("fsdp") % 2).astype(jnp.int32).reshape(1)
+    return gate(odd, x, mine, other.astype(f32), query_proj, taps_dft, inverse)
 
 
 def solution(mesh):

time: 78.7 us -> 66.9 us (0.85)
  waiting for transfers between devices: 24.2 us -> 16.5 us
  blocking collectives: 37.2 us -> 31.1 us
  starting transfers between devices: 9.39 us -> 10.9 us
    ppermute x1, waiting for transfers between devices: 24.2 us -> 10.7 us  [per_device(): earlier = lax.ppermute(mixed, 'seq', [(i, i + 1) for i in range(steps - 1)])]
    all_to_all x1, blocking collectives: 37.2 us -> 31.1 us  [exchange(): lax.all_to_all(copies, 'fsdp', 0, 0, axis_index_groups=groups, tiled=True)]
    all_to_all x1, waiting for transfers between devices: 0.01 us -> 5.84 us  [exchange(): lax.all_to_all(copies, 'fsdp', 0, 0, axis_index_groups=groups, tiled=True)]
    ppermute x0 -> x1, starting transfers between devices: none -> 1.91 us  [per_device(): other = lax.ppermute(mine, 'fsdp', [(i, i ^ 1) for i in range(peers)])]
    convert_element_type x2 -> x3, other arithmetic: 2.31 us -> 1.02 us  [the longest x1 0.84 us: per_device(): mine = exchange((filters * SCALE).astype(WIRE), far)]
    unnamed x16 -> x12, local copies, waits for them, and re-layouts: 0.04 us -> 1 us
    convert_element_type x1, other arithmetic: 0.19 us -> 1.07 us  [per_device(): mixed = (key_proj.astype(f32) * value_proj.astype(f32)).astype(jnp.bfloat16)]
  transfers between devices with their start and end apart: 2 -> 3, of which waited for: 1 -> 2; matrix products, arithmetic and copies ran while one was open for 0% -> 2% of each run, Pallas kernels for 1% -> 1%
where the time goes in v5:
time: 66.9 us; the launch traced here: 66.6 us
  blocking collectives  31.1 us (46%)
  waiting for transfers between devices  16.5 us (25%)
  starting transfers between devices  10.9 us (16%)
  Pallas kernels  4.08 us (6%)
  other arithmetic  2.09 us (3%)
  local copies, waits for them, and re-layouts  1.82 us (3%)
    all_to_all x1, blocking collectives, exchange(): lax.all_to_all(copies, 'fsdp', 0, 0, axis_index_groups=groups, tiled=True)  31.1 us
    ppermute x1, waiting for transfers between devices, per_device(): earlier = lax.ppermute(mixed, 'seq', [(i, i + 1) for i in range(steps - 1)])  10.7 us
    all_to_all x1, waiting for transfers between devices, exchange(): lax.all_to_all(copies, 'fsdp', 0, 0, axis_index_groups=groups, tiled=True)  5.84 us
    all_to_all x1, starting transfers between devices, exchange(): lax.all_to_all(copies, 'fsdp', 0, 0, axis_index_groups=groups, tiled=True)  5.57 us
    ppermute x1, starting transfers between devices, per_device(): earlier = lax.ppermute(mixed, 'seq', [(i, i + 1) for i in range(steps - 1)])  3.39 us
    pallas_call x1, Pallas kernels, gate(): pl.pallas_call(gate_kernel, in_specs=[pl.BlockSpec(memory_space=pltpu.SME...  3.08 us
    ppermute x1, starting transfers between devices, per_device(): other = lax.ppermute(mine, 'fsdp', [(i, i ^ 1) for i in range(peers)])  1.91 us
  transfers between devices with their start and end apart: 3, of which 2 were waited for; matrix products, arithmetic and copies ran while one was open for 2% of the time, Pallas kernels for 1%

profile of v5, /device:TPU:8, one launch (start us, length us, event | category | flops | bytes accessed | tf_op | source)
XLA Modules:
  0.0 66.6 jit_solution(17806547466020485341)
XLA Ops:
  0.0 0.0 copy-start
  0.0 0.8 %multiply_convert_fusion.1 = f16[32,128]{1,0:T(8,128)(2,1)S(1)} fusion(f32[32,128]{1,0:T(8,128)} %param.10), kind=kLoop, calls=%fused_computation.1 | loop fusion | flops 8192 | bytes 24576 | tf_op jit(solution)/shard_map/convert_element_type | solution.py:115
  0.9 31.1 %all_to_all.10 = f16[12,32,128]{2,1,0:T(8,128)(2,1)S(1)} all-to-all(f16[12,32,128]{2,1,0:T(8,128)(2,1)S(1)} %broadcast_in_dim.6), channel_id=1, replica_groups={{0,64,128,192,256,320,384,448,512,576,640,704},{8,72,136,200,264,328,39..., dimensions={0} | all-to-all | bytes 196608 | tf_op jit(solution)/shard_map/all_to_all | solution.py:107
  32.0 0.8 %broadcast_in_dim.7 = f16[4,12,32,128]{3,2,1,0:T(8,128)(2,1)} broadcast(f16[12,32,128]{2,1,0:T(8,128)(2,1)S(1)} %all_to_all.10), dimensions={1,2,3} | broadcast | bytes 491520 | tf_op jit(solution)/shard_map/broadcast_in_dim | solution.py:106
  32.8 5.6 %all-to-all-start.1 = ((f16[4,12,32,128]{3,2,1,0:T(8,128)(2,1)}), f16[4,12,32,128]{3,2,1,0:T(8,128)(2,1)S(1)}, u32[]{:S(2)}, u32[]{:S(2)}) async-start(f16[4,12,32,128]{3,2,1,0:T(8,128)(2,1)} %broadcast_in_dim.7), calls=%async_computation.1 | async-start | bytes 786432 | tf_op jit(solution)/shard_map/all_to_all | solution.py:107
  38.4 0.0 copy-done
  38.4 0.0 copy-done.1
  38.4 1.1 %multiply_convert_fusion = bf16[1,128,3072]{2,1,0:T(8,128)(2,1)} fusion(bf16[1,128,3072]{2,1,0:T(8,128)(2,1)S(1)} %copy-done, bf16[1,128,3072]{2,1,0:T(8,128)(2,1)S(1)} %copy-done.1), kind=kLoop, calls=%fused_computation | loop fusion | flops 1572864 | bytes 2359296 | tf_op jit(solution)/shard_map/convert_element_type | solution.py:116
  39.4 3.4 %collective-permute-start = (bf16[1,128,3072]{2,1,0:T(8,128)(2,1)}, bf16[1,128,3072]{2,1,0:T(8,128)(2,1)S(1)}, u32[]{:S(2)}, u32[]{:S(2)}) collective-permute-start(bf16[1,128,3072]{2,1,0:T(8,128)(2,1)} %multiply_convert_fusion), channel_id=1, source_target_pairs={{0,1},{1,2},{2,3},{3,4},{4,5},{5,6},{6,7},{8,9},{9,10},{10,11},{11... | collective-permute-start | bytes 2359304 | tf_op jit(solution)/shard_map/ppermute | solution.py:117
  42.8 5.8 %all-to-all-done.1 = f16[4,12,32,128]{3,2,1,0:T(8,128)(2,1)S(1)} async-done(((f16[4,12,32,128]{3,2,1,0:T(8,128)(2,1)}), f16[4,12,32,128]{3,2,1,0:T(8,128)(2,1)S(1)}, u32[]{:S(2)}, u32[]{:S(2)}) %all-to-all-start.1) | async-done | bytes 393248 | tf_op jit(solution)/shard_map/all_to_all | solution.py:107
  48.7 1.9 %collective-permute-start.1 = (f16[4,12,32,128]{3,2,1,0:T(8,128)(2,1)S(1)}, f16[4,12,32,128]{3,2,1,0:T(8,128)(2,1)S(1)}, u32[]{:S(2)}, u32[]{:S(2)}) collective-permute-start(f16[4,12,32,128]{3,2,1,0:T(8,128)(2,1)S(1)} %all-to-all-done.1), channel_id=1, source_target_pairs={{0,8},{8,0},{16,24},{24,16},{32,40},{40,32},{48,56},{56,48},{64,72... | collective-permute-start | bytes 1179656 | tf_op jit(solution)/shard_map/ppermute | solution.py:120
  50.6 10.7 %collective-permute-done.prev_ref = bf16[1,128,3072]{2,1,0:T(8,128)(2,1)S(1)} collective-permute-done((bf16[1,128,3072]{2,1,0:T(8,128)(2,1)}, bf16[1,128,3072]{2,1,0:T(8,128)(2,1)S(1)}, u32[]{:S(2)}, u32[]{:S(2)}) %collective-permute-start) | collective-permute-done | bytes 786464 | tf_op jit(solution)/shard_map/ppermute | solution.py:117
  61.3 0.0 copy-done.3
  61.3 1.0 %spectrum.1.x_ref = f32[256,3072]{1,0:T(8,128)S(1)} custom-call(bf16[1,128,3072]{2,1,0:T(8,128)(2,1)S(1)} %collective-permute-done.prev_ref, bf16[1,128,3072]{2,1,0:T(8,128)(2,1)S(1)} %copy-done.1, bf16[1,128,3072]{2,1,0:T(8,128)(2,1)S(1)} %copy-done, bf16[256,512]{1,0:T(8,128)(2,1)S(1)} %copy-done.3), custom_call_target="tpu_custom_call" | custom-call | tf_op jit(solution)/shard_map/spectrum/pallas_call | solution.py:74
  62.3 0.0 copy-start.2
  62.3 0.0 copy-start.4
  62.3 0.0 copy-start.5
  62.3 0.1 convert_element_type.22.mine_ref
  62.4 0.0 collective-permute-done.1
  62.4 0.1 convert_element_type.23.other_ref
  62.5 0.9 %copy-done.2 = bf16[1,128,3072]{2,1,0:T(8,128)(2,1)S(1)} copy-done((bf16[1,128,3072]{2,1,0:T(8,128)(2,1)S(1)}, bf16[1,128,3072]{2,1,0:T(8,128)(2,1)}, u32[]{:S(2)}) %copy-start.2) | copy-done | bytes 786456
  63.4 0.1 copy-done.4
  63.5 0.0 copy-done.5
  63.5 3.1 %gate.1 = bf16[1,128,3072]{2,1,0:T(8,128)(2,1)} custom-call(s32[1]{0:T(128)} %bitcast.odd_ref, f32[256,3072]{1,0:T(8,128)S(1)} %spectrum.1.x_ref, f32[4,12,32,128]{3,2,1,0:T(8,128)S(1)} %convert_element_type.22.mine_ref, f32[4,12,32,128]{3,2,1,0:T(8,128)S(1)} %convert_element_type.23.other_ref, bf16[1,128,3072]{2,1,0:T(8,128)(2,1)S(1)} %copy-done.2, ...), custom_call_target="tpu_custom_call" | custom-call | tf_op jit(solution)/shard_map/gate/pallas_call | solution.py:85
  (3 shorter events, 0.0 us)
Async XLA Ops:
  0.0 38.4 %copy-start = (bf16[1,128,3072]{2,1,0:T(8,128)(2,1)S(1)}, bf16[1,128,3072]{2,1,0:T(8,128)(2,1)}, u32[]{:S(2)}) copy-start(bf16[1,128,3072]{2,1,0:T(8,128)(2,1)} %value_ref.1) | copy-start | bytes 2359300
  0.0 38.4 %copy-start.1 = (bf16[1,128,3072]{2,1,0:T(8,128)(2,1)S(1)}, bf16[1,128,3072]{2,1,0:T(8,128)(2,1)}, u32[]{:S(2)}) copy-start(bf16[1,128,3072]{2,1,0:T(8,128)(2,1)} %key_ref.1) | copy-start | bytes 2359300
  32.8 28.5 %copy-start.3 = (bf16[256,512]{1,0:T(8,128)(2,1)S(1)}, bf16[256,512]{1,0:T(8,128)(2,1)}, u32[]{:S(2)}) copy-start(bf16[256,512]{1,0:T(8,128)(2,1)} %constant.26.clone.f_ref) | copy-start | bytes 786436
  32.8 15.9 %all-to-all-start.1 = ((f16[4,12,32,128]{3,2,1,0:T(8,128)(2,1)}), f16[4,12,32,128]{3,2,1,0:T(8,128)(2,1)S(1)}, u32[]{:S(2)}, u32[]{:S(2)}) async-start(f16[4,12,32,128]{3,2,1,0:T(8,128)(2,1)} %broadcast_in_dim.7), calls=%async_computation.1 | async-start | bytes 786432 | tf_op jit(solution)/shard_map/all_to_all | solution.py:107
  39.4 21.8 %collective-permute-start = (bf16[1,128,3072]{2,1,0:T(8,128)(2,1)}, bf16[1,128,3072]{2,1,0:T(8,128)(2,1)S(1)}, u32[]{:S(2)}, u32[]{:S(2)}) collective-permute-start(bf16[1,128,3072]{2,1,0:T(8,128)(2,1)} %multiply_convert_fusion), channel_id=1, source_target_pairs={{0,1},{1,2},{2,3},{3,4},{4,5},{5,6},{6,7},{8,9},{9,10},{10,11},{11... | collective-permute-start | bytes 2359304 | tf_op jit(solution)/shard_map/ppermute | solution.py:117
  48.7 13.7 %collective-permute-start.1 = (f16[4,12,32,128]{3,2,1,0:T(8,128)(2,1)S(1)}, f16[4,12,32,128]{3,2,1,0:T(8,128)(2,1)S(1)}, u32[]{:S(2)}, u32[]{:S(2)}) collective-permute-start(f16[4,12,32,128]{3,2,1,0:T(8,128)(2,1)S(1)} %all-to-all-done.1), channel_id=1, source_target_pairs={{0,8},{8,0},{16,24},{24,16},{32,40},{40,32},{48,56},{56,48},{64,72... | collective-permute-start | bytes 1179656 | tf_op jit(solution)/shard_map/ppermute | solution.py:120
  62.3 1.1 %copy-start.2 = (bf16[1,128,3072]{2,1,0:T(8,128)(2,1)S(1)}, bf16[1,128,3072]{2,1,0:T(8,128)(2,1)}, u32[]{:S(2)}) copy-start(bf16[1,128,3072]{2,1,0:T(8,128)(2,1)} %query_ref.1) | copy-start | bytes 2359300
  62.3 1.2 %copy-start.4 = (bf16[512,256]{1,0:T(8,128)(2,1)S(1)}, bf16[512,256]{1,0:T(8,128)(2,1)}, u32[]{:S(2)}) copy-start(bf16[512,256]{1,0:T(8,128)(2,1)} %constant.27.clone.f_ref) | copy-start | bytes 786436
  62.3 1.2 %copy-start.5 = (bf16[256,256]{1,0:T(8,128)(2,1)S(1)}, bf16[256,256]{1,0:T(8,128)(2,1)}, u32[]{:S(2)}) copy-start(bf16[256,256]{1,0:T(8,128)(2,1)} %constant.28.clone.g_ref) | copy-start | bytes 393220

commit v6 on v5

--- a/solution.py
+++ b/solution.py
@@ -37,10 +37,18 @@
     )
 
 
-def spectrum_kernel(prev_ref, key_ref, value_ref, f_ref, x_ref):
+def spectrum_kernel(prev_ref, key_ref, value_ref, f_ref, x_ref, prev, key, value, sems):
+    copies = [
+        pltpu.make_async_copy(source, target, sems.at[i])
+        for i, (source, target) in enumerate(((key_ref, key), (value_ref, value), (prev_ref, prev)))
+    ]
+    for copy in copies:
+        copy.start()
+    for copy in copies:
+        copy.wait()
     f32 = jnp.float32
-    mixed = (key_ref[0].astype(f32) * value_ref[0].astype(f32)).astype(jnp.bfloat16)
-    window = jnp.concatenate([prev_ref[0], mixed], axis=0)
+    mixed = (key[0].astype(f32) * value[0].astype(f32)).astype(jnp.bfloat16)
+    window = jnp.concatenate([prev[0], mixed], axis=0)
     x_ref[...] = dot(f_ref[...], jnp.concatenate([window, window], axis=0))
 
 
@@ -73,9 +81,10 @@
 def spectrum(prev, key, value, forward):
     return pl.pallas_call(
         spectrum_kernel,
-        in_specs=[VMEM] * 4,
+        in_specs=[pl.BlockSpec(memory_space=pl.ANY)] * 3 + [VMEM],
         out_specs=VMEM,
         out_shape=jax.ShapeDtypeStruct((forward.shape[0], key.shape[2]), jnp.float32),
+        scratch_shapes=[pltpu.VMEM(key.shape, key.dtype)] * 3 + [pltpu.SemaphoreType.DMA((3,))],
         compiler_params=PARAMS,
         name="spectrum",
     )(prev, key, value, forward)
@@ -102,8 +111,7 @@
     return far, near
 
 
-def exchange(piece, groups):
-    copies = jnp.broadcast_to(piece, (len(groups[0]),) + piece.shape)
+def exchange(copies, groups):
     return lax.all_to_all(copies, "fsdp", 0, 0, axis_index_groups=groups, tiled=True)
 
 
@@ -112,10 +120,12 @@
     peers, steps = lax.axis_size("fsdp"), lax.axis_size("seq")
     window_dft, taps_dft, inverse = transforms(filters.shape[1])
     far, near = stage_groups(peers)
-    mine = exchange((filters * SCALE).astype(WIRE), far)
+    copy = lax.broadcasted_iota(jnp.int32, (len(far[0]),) + filters.shape, 0)
+    scale = SCALE + jnp.minimum(copy, 0).astype(f32)
+    mine = exchange((filters[None] * scale).astype(WIRE), far)
     mixed = (key_proj.astype(f32) * value_proj.astype(f32)).astype(jnp.bfloat16)
     earlier = lax.ppermute(mixed, "seq", [(i, i + 1) for i in range(steps - 1)])
-    mine = exchange(mine, near)
+    mine = exchange(jnp.broadcast_to(mine, (NEAR,) + mine.shape), near)
     x = spectrum(earlier, key_proj, value_proj, window_dft)
     other = lax.ppermute(mine, "fsdp", [(i, i ^ 1) for i in range(peers)])
     mine = mine.astype(f32)

time: 66.9 us -> 67.2 us (level)
  transfers between devices with their start and end apart: 3 -> 3, of which waited for: 2 -> 2; matrix products, arithmetic and copies ran while one was open for 2% -> 2% of each run, Pallas kernels for 1% -> 2%
where the time goes in v6:
time: 67.2 us; the launch traced here: 66.8 us
  blocking collectives  31.1 us (46%)
  waiting for transfers between devices  16.5 us (25%)
  starting transfers between devices  10.9 us (16%)
  Pallas kernels  4.27 us (6%)
  other arithmetic  2.17 us (3%)
  local copies, waits for them, and re-layouts  1.8 us (3%)
    all_to_all x1, blocking collectives, exchange(): lax.all_to_all(copies, 'fsdp', 0, 0, axis_index_groups=groups, tiled=True)  31.1 us
    ppermute x1, waiting for transfers between devices, per_device(): earlier = lax.ppermute(mixed, 'seq', [(i, i + 1) for i in range(steps - 1)])  10.7 us
    all_to_all x1, waiting for transfers between devices, exchange(): lax.all_to_all(copies, 'fsdp', 0, 0, axis_index_groups=groups, tiled=True)  5.84 us
    all_to_all x1, starting transfers between devices, exchange(): lax.all_to_all(copies, 'fsdp', 0, 0, axis_index_groups=groups, tiled=True)  5.57 us
    ppermute x1, starting transfers between devices, per_device(): earlier = lax.ppermute(mixed, 'seq', [(i, i + 1) for i in range(steps - 1)])  3.39 us
    pallas_call x1, Pallas kernels, gate(): pl.pallas_call(gate_kernel, in_specs=[pl.BlockSpec(memory_space=pltpu.SME...  3.09 us
    ppermute x1, starting transfers between devices, per_device(): other = lax.ppermute(mine, 'fsdp', [(i, i ^ 1) for i in range(peers)])  1.91 us
  transfers between devices with their start and end apart: 3, of which 2 were waited for; matrix products, arithmetic and copies ran while one was open for 2% of the time, Pallas kernels for 2%

profile of v6, /device:TPU:8, one launch (start us, length us, event | category | flops | bytes accessed | tf_op | source)
XLA Modules:
  0.0 66.8 jit_solution(8054631346806043772)
XLA Ops:
  0.0 0.0 copy-start
  0.0 0.9 %multiply_convert_fusion.1 = f16[12,32,128]{2,1,0:T(8,128)(2,1)S(1)} fusion(f32[12]{0:T(128)S(1)} %convert_add_fusion, f32[32,128]{1,0:T(8,128)} %param.10), kind=kLoop, calls=%fused_computation.1 | loop fusion | flops 98304 | bytes 114736 | tf_op jit(solution)/shard_map/convert_element_type | solution.py:125
  0.9 31.1 %all_to_all.10 = f16[12,32,128]{2,1,0:T(8,128)(2,1)S(1)} all-to-all(f16[12,32,128]{2,1,0:T(8,128)(2,1)S(1)} %multiply_convert_fusion.1), channel_id=1, replica_groups={{0,64,128,192,256,320,384,448,512,576,640,704},{8,72,136,200,264,328,39..., dimensions={0} | all-to-all | bytes 196608 | tf_op jit(solution)/shard_map/all_to_all | solution.py:115
  32.1 0.8 %broadcast_in_dim.4 = f16[4,12,32,128]{3,2,1,0:T(8,128)(2,1)} broadcast(f16[12,32,128]{2,1,0:T(8,128)(2,1)S(1)} %all_to_all.10), dimensions={1,2,3} | broadcast | bytes 491520 | tf_op jit(solution)/shard_map/broadcast_in_dim | solution.py:128
  32.9 5.6 %all-to-all-start.1 = ((f16[4,12,32,128]{3,2,1,0:T(8,128)(2,1)}), f16[4,12,32,128]{3,2,1,0:T(8,128)(2,1)S(1)}, u32[]{:S(2)}, u32[]{:S(2)}) async-start(f16[4,12,32,128]{3,2,1,0:T(8,128)(2,1)} %broadcast_in_dim.4), calls=%async_computation.1 | async-start | bytes 786432 | tf_op jit(solution)/shard_map/all_to_all | solution.py:115
  38.4 0.0 copy-done
  38.4 0.0 copy-done.1
  38.4 1.1 %multiply_convert_fusion = bf16[1,128,3072]{2,1,0:T(8,128)(2,1)} fusion(bf16[1,128,3072]{2,1,0:T(8,128)(2,1)S(1)} %copy-done, bf16[1,128,3072]{2,1,0:T(8,128)(2,1)S(1)} %copy-done.1), kind=kLoop, calls=%fused_computation | loop fusion | flops 1572864 | bytes 2359296 | tf_op jit(solution)/shard_map/convert_element_type | solution.py:126
  39.5 3.4 %collective-permute-start = (bf16[1,128,3072]{2,1,0:T(8,128)(2,1)}, bf16[1,128,3072]{2,1,0:T(8,128)(2,1)S(1)}, u32[]{:S(2)}, u32[]{:S(2)}) collective-permute-start(bf16[1,128,3072]{2,1,0:T(8,128)(2,1)} %multiply_convert_fusion), channel_id=1, source_target_pairs={{0,1},{1,2},{2,3},{3,4},{4,5},{5,6},{6,7},{8,9},{9,10},{10,11},{11... | collective-permute-start | bytes 2359304 | tf_op jit(solution)/shard_map/ppermute | solution.py:127
  42.9 5.8 %all-to-all-done.1 = f16[4,12,32,128]{3,2,1,0:T(8,128)(2,1)S(1)} async-done(((f16[4,12,32,128]{3,2,1,0:T(8,128)(2,1)}), f16[4,12,32,128]{3,2,1,0:T(8,128)(2,1)S(1)}, u32[]{:S(2)}, u32[]{:S(2)}) %all-to-all-start.1) | async-done | bytes 393248 | tf_op jit(solution)/shard_map/all_to_all | solution.py:115
  48.7 1.9 %collective-permute-start.1 = (f16[4,12,32,128]{3,2,1,0:T(8,128)(2,1)S(1)}, f16[4,12,32,128]{3,2,1,0:T(8,128)(2,1)S(1)}, u32[]{:S(2)}, u32[]{:S(2)}) collective-permute-start(f16[4,12,32,128]{3,2,1,0:T(8,128)(2,1)S(1)} %all-to-all-done.1), channel_id=1, source_target_pairs={{0,8},{8,0},{16,24},{24,16},{32,40},{40,32},{48,56},{56,48},{64,72... | collective-permute-start | bytes 1179656 | tf_op jit(solution)/shard_map/ppermute | solution.py:130
  50.7 10.7 %collective-permute-done.prev_ref = bf16[1,128,3072]{2,1,0:T(8,128)(2,1)S(1)} collective-permute-done((bf16[1,128,3072]{2,1,0:T(8,128)(2,1)}, bf16[1,128,3072]{2,1,0:T(8,128)(2,1)S(1)}, u32[]{:S(2)}, u32[]{:S(2)}) %collective-permute-start) | collective-permute-done | bytes 786464 | tf_op jit(solution)/shard_map/ppermute | solution.py:127
  61.3 0.0 copy-done.3
  61.3 1.2 %spectrum.1.x_ref = f32[256,3072]{1,0:T(8,128)S(1)} custom-call(bf16[1,128,3072]{2,1,0:T(8,128)(2,1)S(1)} %collective-permute-done.prev_ref, bf16[1,128,3072]{2,1,0:T(8,128)(2,1)S(1)} %copy-done.1, bf16[1,128,3072]{2,1,0:T(8,128)(2,1)S(1)} %copy-done, bf16[256,512]{1,0:T(8,128)(2,1)S(1)} %copy-done.3), custom_call_target="tpu_custom_call" | custom-call | tf_op jit(solution)/shard_map/spectrum/pallas_call | solution.py:82
  62.5 0.0 copy-start.2
  62.5 0.0 copy-start.4
  62.6 0.0 copy-start.5
  62.6 0.1 convert_element_type.27.mine_ref
  62.7 0.0 collective-permute-done.1
  62.7 0.1 convert_element_type.28.other_ref
  62.8 0.9 %copy-done.2 = bf16[1,128,3072]{2,1,0:T(8,128)(2,1)S(1)} copy-done((bf16[1,128,3072]{2,1,0:T(8,128)(2,1)S(1)}, bf16[1,128,3072]{2,1,0:T(8,128)(2,1)}, u32[]{:S(2)}) %copy-start.2) | copy-done | bytes 786456
  63.7 0.1 copy-done.4
  63.7 0.0 copy-done.5
  63.8 3.1 %gate.1 = bf16[1,128,3072]{2,1,0:T(8,128)(2,1)} custom-call(s32[1]{0:T(128)} %bitcast.odd_ref, f32[256,3072]{1,0:T(8,128)S(1)} %spectrum.1.x_ref, f32[4,12,32,128]{3,2,1,0:T(8,128)S(1)} %convert_element_type.27.mine_ref, f32[4,12,32,128]{3,2,1,0:T(8,128)S(1)} %convert_element_type.28.other_ref, bf16[1,128,3072]{2,1,0:T(8,128)(2,1)S(1)} %copy-done.2, ...), custom_call_target="tpu_custom_call" | custom-call | tf_op jit(solution)/shard_map/gate/pallas_call | solution.py:94
  (3 shorter events, 0.0 us)
Async XLA Ops:
  0.0 38.4 %copy-start = (bf16[1,128,3072]{2,1,0:T(8,128)(2,1)S(1)}, bf16[1,128,3072]{2,1,0:T(8,128)(2,1)}, u32[]{:S(2)}) copy-start(bf16[1,128,3072]{2,1,0:T(8,128)(2,1)} %value_ref.1) | copy-start | bytes 2359300
  0.0 38.4 %copy-start.1 = (bf16[1,128,3072]{2,1,0:T(8,128)(2,1)S(1)}, bf16[1,128,3072]{2,1,0:T(8,128)(2,1)}, u32[]{:S(2)}) copy-start(bf16[1,128,3072]{2,1,0:T(8,128)(2,1)} %key_ref.1) | copy-start | bytes 2359300
  32.9 28.5 %copy-start.3 = (bf16[256,512]{1,0:T(8,128)(2,1)S(1)}, bf16[256,512]{1,0:T(8,128)(2,1)}, u32[]{:S(2)}) copy-start(bf16[256,512]{1,0:T(8,128)(2,1)} %constant.27.clone.f_ref) | copy-start | bytes 786436
  32.9 15.9 %all-to-all-start.1 = ((f16[4,12,32,128]{3,2,1,0:T(8,128)(2,1)}), f16[4,12,32,128]{3,2,1,0:T(8,128)(2,1)S(1)}, u32[]{:S(2)}, u32[]{:S(2)}) async-start(f16[4,12,32,128]{3,2,1,0:T(8,128)(2,1)} %broadcast_in_dim.4), calls=%async_computation.1 | async-start | bytes 786432 | tf_op jit(solution)/shard_map/all_to_all | solution.py:115
  39.5 21.8 %collective-permute-start = (bf16[1,128,3072]{2,1,0:T(8,128)(2,1)}, bf16[1,128,3072]{2,1,0:T(8,128)(2,1)S(1)}, u32[]{:S(2)}, u32[]{:S(2)}) collective-permute-start(bf16[1,128,3072]{2,1,0:T(8,128)(2,1)} %multiply_convert_fusion), channel_id=1, source_target_pairs={{0,1},{1,2},{2,3},{3,4},{4,5},{5,6},{6,7},{8,9},{9,10},{10,11},{11... | collective-permute-start | bytes 2359304 | tf_op jit(solution)/shard_map/ppermute | solution.py:127
  48.7 13.9 %collective-permute-start.1 = (f16[4,12,32,128]{3,2,1,0:T(8,128)(2,1)S(1)}, f16[4,12,32,128]{3,2,1,0:T(8,128)(2,1)S(1)}, u32[]{:S(2)}, u32[]{:S(2)}) collective-permute-start(f16[4,12,32,128]{3,2,1,0:T(8,128)(2,1)S(1)} %all-to-all-done.1), channel_id=1, source_target_pairs={{0,8},{8,0},{16,24},{24,16},{32,40},{40,32},{48,56},{56,48},{64,72... | collective-permute-start | bytes 1179656 | tf_op jit(solution)/shard_map/ppermute | solution.py:130
  62.5 1.1 %copy-start.2 = (bf16[1,128,3072]{2,1,0:T(8,128)(2,1)S(1)}, bf16[1,128,3072]{2,1,0:T(8,128)(2,1)}, u32[]{:S(2)}) copy-start(bf16[1,128,3072]{2,1,0:T(8,128)(2,1)} %query_ref.1) | copy-start | bytes 2359300
  62.5 1.2 %copy-start.4 = (bf16[512,256]{1,0:T(8,128)(2,1)S(1)}, bf16[512,256]{1,0:T(8,128)(2,1)}, u32[]{:S(2)}) copy-start(bf16[512,256]{1,0:T(8,128)(2,1)} %constant.28.clone.f_ref) | copy-start | bytes 786436
  62.6 1.2 %copy-start.5 = (bf16[256,256]{1,0:T(8,128)(2,1)S(1)}, bf16[256,256]{1,0:T(8,128)(2,1)}, u32[]{:S(2)}) copy-start(bf16[256,256]{1,0:T(8,128)(2,1)} %constant.29.clone.g_ref) | copy-start | bytes 393220

commit v7 on v6

--- a/solution.py
+++ b/solution.py
@@ -37,29 +37,49 @@
     )
 
 
-def spectrum_kernel(prev_ref, key_ref, value_ref, f_ref, x_ref, prev, key, value, sems):
-    copies = [
-        pltpu.make_async_copy(source, target, sems.at[i])
-        for i, (source, target) in enumerate(((key_ref, key), (value_ref, value), (prev_ref, prev)))
-    ]
+NEAR = 4
+CHUNKS = 3
+
+
+def near_order(members):
+    return [members // 2] + [i for i in range(members) if i != members // 2]
+
+
+def far_order(members):
+    rows = members // CHUNKS
+    return sorted(range(members), key=lambda i: (-(i % CHUNKS), (i // CHUNKS - rows // 2) % rows))
+
+
+def stage_groups(peers):
+    index = np.arange(peers).reshape(-1, NEAR, 2)
+    chunks = index.shape[0]
+    far = [index[far_order(chunks), near, core].tolist() for near in range(NEAR) for core in range(2)]
+    near = [index[chunk, near_order(NEAR), core].tolist() for chunk in range(chunks) for core in range(2)]
+    return far, near
+
+
+def spectrum_kernel(prev_ref, cur_ref, query_ref, f_ref, x_ref, kept_ref, prev, cur, sems):
+    pairs = ((cur_ref, cur), (prev_ref, prev), (query_ref, kept_ref))
+    copies = [pltpu.make_async_copy(source, target, sems.at[i]) for i, (source, target) in enumerate(pairs)]
     for copy in copies:
         copy.start()
-    for copy in copies:
+    for copy in copies[:2]:
         copy.wait()
-    f32 = jnp.float32
-    mixed = (key[0].astype(f32) * value[0].astype(f32)).astype(jnp.bfloat16)
-    window = jnp.concatenate([prev[0], mixed], axis=0)
+    window = jnp.concatenate([prev[0], cur[0]], axis=0)
     x_ref[...] = dot(f_ref[...], jnp.concatenate([window, window], axis=0))
+    copies[2].wait()
 
 
 def gate_kernel(odd_ref, x_ref, mine_ref, other_ref, query_ref, f_ref, g_ref, out_ref):
     f32, bf16 = jnp.float32, jnp.bfloat16
-    taps = mine_ref.shape[-1]
+    near, far, _, taps = mine_ref.shape
     odd = odd_ref[0] == 1
     pieces = []
-    for i in range(mine_ref.shape[0]):
-        mine, other = mine_ref[i], other_ref[i]
-        pieces += [jnp.where(odd, other, mine), jnp.where(odd, mine, other)]
+    for i in range(near):
+        at = near_order(near).index(i)
+        for ref, twin in ((mine_ref, other_ref), (other_ref, mine_ref)):
+            piece = jnp.where(odd, twin[at], ref[at])
+            pieces.append(jnp.stack([piece[far_order(far).index(j)] for j in range(far)]))
     w = jnp.concatenate(pieces, axis=1).reshape(-1, taps)
     wh = w.astype(bf16)
     wl = (w - wh.astype(f32)).astype(bf16)
@@ -78,16 +98,17 @@
 PARAMS = pltpu.CompilerParams(vmem_limit_bytes=24 << 20)
 
 
-def spectrum(prev, key, value, forward):
+def spectrum(prev, cur, query, forward):
+    x = jax.ShapeDtypeStruct((forward.shape[0], cur.shape[2]), jnp.float32)
     return pl.pallas_call(
         spectrum_kernel,
         in_specs=[pl.BlockSpec(memory_space=pl.ANY)] * 3 + [VMEM],
-        out_specs=VMEM,
-        out_shape=jax.ShapeDtypeStruct((forward.shape[0], key.shape[2]), jnp.float32),
-        scratch_shapes=[pltpu.VMEM(key.shape, key.dtype)] * 3 + [pltpu.SemaphoreType.DMA((3,))],
+        out_specs=[VMEM] * 2,
+        out_shape=[x, jax.ShapeDtypeStruct(query.shape, query.dtype)],
+        scratch_shapes=[pltpu.VMEM(cur.shape, cur.dtype)] * 2 + [pltpu.SemaphoreType.DMA((3,))],
         compiler_params=PARAMS,
         name="spectrum",
-    )(prev, key, value, forward)
+    )(prev, cur, query, forward)
 
 
 def gate(odd, x, mine, other, query, forward, inverse):
@@ -101,16 +122,6 @@
     )(odd, x, mine, other, query, forward, inverse)
 
 
-NEAR = 4
-
-
-def stage_groups(peers):
-    index = np.arange(peers).reshape(-1, NEAR, 2)
-    far = [index[:, near, core].tolist() for near in range(NEAR) for core in range(2)]
-    near = [index[chunk, :, core].tolist() for chunk in range(index.shape[0]) for core in range(2)]
-    return far, near
-
-
 def exchange(copies, groups):
     return lax.all_to_all(copies, "fsdp", 0, 0, axis_index_groups=groups, tiled=True)
 
@@ -120,17 +131,16 @@
     peers, steps = lax.axis_size("fsdp"), lax.axis_size("seq")
     window_dft, taps_dft, inverse = transforms(filters.shape[1])
     far, near = stage_groups(peers)
-    copy = lax.broadcasted_iota(jnp.int32, (len(far[0]),) + filters.shape, 0)
-    scale = SCALE + jnp.minimum(copy, 0).astype(f32)
-    mine = exchange((filters[None] * scale).astype(WIRE), far)
+    mine = (filters * SCALE).astype(WIRE)
+    mine = exchange(jnp.broadcast_to(mine, (len(far[0]),) + mine.shape), far)
     mixed = (key_proj.astype(f32) * value_proj.astype(f32)).astype(jnp.bfloat16)
     earlier = lax.ppermute(mixed, "seq", [(i, i + 1) for i in range(steps - 1)])
     mine = exchange(jnp.broadcast_to(mine, (NEAR,) + mine.shape), near)
-    x = spectrum(earlier, key_proj, value_proj, window_dft)
+    x, query = spectrum(earlier, mixed, query_proj, window_dft)
     other = lax.ppermute(mine, "fsdp", [(i, i ^ 1) for i in range(peers)])
     mine = mine.astype(f32)
     odd = (lax.axis_index("fsdp") % 2).astype(jnp.int32).reshape(1)
-    return gate(odd, x, mine, other.astype(f32), query_proj, taps_dft, inverse)
+    return gate(odd, x, mine, other.astype(f32), query, taps_dft, inverse)
 
 
 def solution(mesh):

time: 67.2 us -> 61.1 us (0.909)
  the two profiles are of different devices: /device:TPU:8 before, /device:TPU:40 now
where the time goes in v7:
time: 61.1 us; the launch traced here: 60.8 us
  blocking collectives  24.9 us (41%)
  waiting for transfers between devices  16.2 us (27%)
  starting transfers between devices  11.5 us (19%)
  Pallas kernels  4.1 us (7%)
  other arithmetic  2.29 us (4%)
  local copies, waits for them, and re-layouts  1.61 us (3%)
    all_to_all x1, blocking collectives, exchange(): lax.all_to_all(copies, 'fsdp', 0, 0, axis_index_groups=groups, tiled=True)  24.9 us
    ppermute x1, waiting for transfers between devices, per_device(): earlier = lax.ppermute(mixed, 'seq', [(i, i + 1) for i in range(steps - 1)])  13.6 us
    all_to_all x1, starting transfers between devices, exchange(): lax.all_to_all(copies, 'fsdp', 0, 0, axis_index_groups=groups, tiled=True)  6.21 us
    ppermute x1, starting transfers between devices, per_device(): earlier = lax.ppermute(mixed, 'seq', [(i, i + 1) for i in range(steps - 1)])  3.4 us
    pallas_call x1, Pallas kernels, gate(): pl.pallas_call(gate_kernel, in_specs=[pl.BlockSpec(memory_space=pltpu.SME...  2.93 us
    all_to_all x1, waiting for transfers between devices, exchange(): lax.all_to_all(copies, 'fsdp', 0, 0, axis_index_groups=groups, tiled=True)  2.66 us
    ppermute x1, starting transfers between devices, per_device(): other = lax.ppermute(mine, 'fsdp', [(i, i ^ 1) for i in range(peers)])  1.91 us
    convert_element_type x1, other arithmetic, per_device(): mixed = (key_proj.astype(f32) * value_proj.astype(f32)).astype(jnp.bfloat16)  1.32 us
  transfers between devices with their start and end apart: 3, of which 2 were waited for; matrix products, arithmetic and copies ran while one was open for 2% of the time, Pallas kernels for 2%

profile of v7, /device:TPU:40, one launch (start us, length us, event | category | flops | bytes accessed | tf_op | source)
XLA Modules:
  0.0 60.8 jit_solution(15247494891841337250)
XLA Ops:
  0.0 0.0 copy-start.4
  0.0 0.8 %multiply_convert_fusion.1 = f16[32,128]{1,0:T(8,128)(2,1)S(1)} fusion(f32[32,128]{1,0:T(8,128)} %param.10), kind=kLoop, calls=%fused_computation.1 | loop fusion | flops 8192 | bytes 24576 | tf_op jit(solution)/shard_map/convert_element_type | solution.py:134
  0.8 24.9 %all_to_all.10 = f16[12,32,128]{2,1,0:T(8,128)(2,1)S(1)} all-to-all(f16[12,32,128]{2,1,0:T(8,128)(2,1)S(1)} %broadcast_in_dim.6), channel_id=1, replica_groups={{512,704,128,320,448,640,64,256,384,576,0,192},{520,712,136,328,456,648..., dimensions={0} | all-to-all | bytes 196608 | tf_op jit(solution)/shard_map/all_to_all | solution.py:126
  25.7 0.8 %broadcast_in_dim.7 = f16[4,12,32,128]{3,2,1,0:T(8,128)(2,1)} broadcast(f16[12,32,128]{2,1,0:T(8,128)(2,1)S(1)} %all_to_all.10), dimensions={1,2,3} | broadcast | bytes 491520 | tf_op jit(solution)/shard_map/broadcast_in_dim | solution.py:138
  26.6 0.0 copy-start
  26.6 0.0 copy-start.1
  26.6 6.2 %all-to-all-start.1 = ((f16[4,12,32,128]{3,2,1,0:T(8,128)(2,1)}), f16[4,12,32,128]{3,2,1,0:T(8,128)(2,1)S(1)}, u32[]{:S(2)}, u32[]{:S(2)}) async-start(f16[4,12,32,128]{3,2,1,0:T(8,128)(2,1)} %broadcast_in_dim.7), calls=%async_computation.1 | async-start | bytes 786432 | tf_op jit(solution)/shard_map/all_to_all | solution.py:126
  32.8 0.0 copy-done.4
  32.8 1.3 %multiply_convert_fusion.cur_ref = bf16[1,128,3072]{2,1,0:T(8,128)(2,1)S(1)} fusion(bf16[1,128,3072]{2,1,0:T(8,128)(2,1)S(1)} %copy-done.4, bf16[1,128,3072]{2,1,0:T(8,128)(2,1)} %param.8), kind=kLoop, calls=%fused_computation | loop fusion | flops 1572864 | bytes 2359296 | tf_op jit(solution)/shard_map/convert_element_type | solution.py:136
  34.1 3.4 %collective-permute-start = (bf16[1,128,3072]{2,1,0:T(8,128)(2,1)S(1)}, bf16[1,128,3072]{2,1,0:T(8,128)(2,1)S(1)}, u32[]{:S(2)}, u32[]{:S(2)}) collective-permute-start(bf16[1,128,3072]{2,1,0:T(8,128)(2,1)S(1)} %multiply_convert_fusion.cur_ref), channel_id=1, source_target_pairs={{0,1},{1,2},{2,3},{3,4},{4,5},{5,6},{6,7},{8,9},{9,10},{10,11},{11... | collective-permute-start | bytes 2359304 | tf_op jit(solution)/shard_map/ppermute | solution.py:137
  37.5 2.7 %all-to-all-done.1 = f16[4,12,32,128]{3,2,1,0:T(8,128)(2,1)S(1)} async-done(((f16[4,12,32,128]{3,2,1,0:T(8,128)(2,1)}), f16[4,12,32,128]{3,2,1,0:T(8,128)(2,1)S(1)}, u32[]{:S(2)}, u32[]{:S(2)}) %all-to-all-start.1) | async-done | bytes 393248 | tf_op jit(solution)/shard_map/all_to_all | solution.py:126
  40.2 1.9 %collective-permute-start.1 = (f16[4,12,32,128]{3,2,1,0:T(8,128)(2,1)S(1)}, f16[4,12,32,128]{3,2,1,0:T(8,128)(2,1)S(1)}, u32[]{:S(2)}, u32[]{:S(2)}) collective-permute-start(f16[4,12,32,128]{3,2,1,0:T(8,128)(2,1)S(1)} %all-to-all-done.1), channel_id=1, source_target_pairs={{0,8},{8,0},{16,24},{24,16},{32,40},{40,32},{48,56},{56,48},{64,72... | collective-permute-start | bytes 1179656 | tf_op jit(solution)/shard_map/ppermute | solution.py:140
  42.1 13.6 %collective-permute-done.prev_ref = bf16[1,128,3072]{2,1,0:T(8,128)(2,1)S(1)} collective-permute-done((bf16[1,128,3072]{2,1,0:T(8,128)(2,1)S(1)}, bf16[1,128,3072]{2,1,0:T(8,128)(2,1)S(1)}, u32[]{:S(2)}, u32[]{:S(2)}) %collective-permute-start) | collective-permute-done | bytes 786464 | tf_op jit(solution)/shard_map/ppermute | solution.py:137
  55.7 0.0 copy-done
  55.7 0.0 copy-done.1
  55.7 1.2 %spectrum.1 = (f32[256,3072]{1,0:T(8,128)S(1)}, bf16[1,128,3072]{2,1,0:T(8,128)(2,1)S(1)}) custom-call(bf16[1,128,3072]{2,1,0:T(8,128)(2,1)S(1)} %collective-permute-done.prev_ref, bf16[1,128,3072]{2,1,0:T(8,128)(2,1)S(1)} %multiply_convert_fusion.cur_ref, bf16[1,128,3072]{2,1,0:T(8,128)(2,1)S(1)} %copy-done, bf16[256,512]{1,0:T(8,128)(2,1)S(1)} %copy-done.1), custom_call_target="tpu_custom_call" | custom-call | tf_op jit(solution)/shard_map/spectrum/pallas_call | solution.py:103
  56.8 0.0 copy-start.2
  56.9 0.0 copy-start.3
  56.9 0.1 convert_element_type.22.mine_ref
  57.0 0.0 collective-permute-done.1
  57.0 0.1 convert_element_type.23.other_ref
  57.1 0.7 %copy-done.2 = bf16[512,256]{1,0:T(8,128)(2,1)S(1)} copy-done((bf16[512,256]{1,0:T(8,128)(2,1)S(1)}, bf16[512,256]{1,0:T(8,128)(2,1)}, u32[]{:S(2)}) %copy-start.2) | copy-done | bytes 262168
  57.8 0.0 copy-done.3
  57.8 2.9 %gate.1 = bf16[1,128,3072]{2,1,0:T(8,128)(2,1)} custom-call(s32[1]{0:T(128)} %bitcast.odd_ref, f32[256,3072]{1,0:T(8,128)S(1)} %get-tuple-element.7.x_ref, f32[4,12,32,128]{3,2,1,0:T(8,128)S(1)} %convert_element_type.22.mine_ref, f32[4,12,32,128]{3,2,1,0:T(8,128)S(1)} %convert_element_type.23.other_ref, ...), custom_call_target="tpu_custom_call" | custom-call | tf_op jit(solution)/shard_map/gate/pallas_call | solution.py:115
  (1 shorter events, 0.0 us)
Async XLA Ops:
  0.0 32.8 %copy-start.4 = (bf16[1,128,3072]{2,1,0:T(8,128)(2,1)S(1)}, bf16[1,128,3072]{2,1,0:T(8,128)(2,1)}, u32[]{:S(2)}) copy-start(bf16[1,128,3072]{2,1,0:T(8,128)(2,1)} %param.9) | copy-start | bytes 2359300
  26.6 29.1 %copy-start = (bf16[1,128,3072]{2,1,0:T(8,128)(2,1)S(1)}, bf16[1,128,3072]{2,1,0:T(8,128)(2,1)}, u32[]{:S(2)}) copy-start(bf16[1,128,3072]{2,1,0:T(8,128)(2,1)} %query_ref.1) | copy-start | bytes 2359300
  26.6 29.1 %copy-start.1 = (bf16[256,512]{1,0:T(8,128)(2,1)S(1)}, bf16[256,512]{1,0:T(8,128)(2,1)}, u32[]{:S(2)}) copy-start(bf16[256,512]{1,0:T(8,128)(2,1)} %constant.26.clone.f_ref) | copy-start | bytes 786436
  26.6 13.6 %all-to-all-start.1 = ((f16[4,12,32,128]{3,2,1,0:T(8,128)(2,1)}), f16[4,12,32,128]{3,2,1,0:T(8,128)(2,1)S(1)}, u32[]{:S(2)}, u32[]{:S(2)}) async-start(f16[4,12,32,128]{3,2,1,0:T(8,128)(2,1)} %broadcast_in_dim.7), calls=%async_computation.1 | async-start | bytes 786432 | tf_op jit(solution)/shard_map/all_to_all | solution.py:126
  34.1 21.6 %collective-permute-start = (bf16[1,128,3072]{2,1,0:T(8,128)(2,1)S(1)}, bf16[1,128,3072]{2,1,0:T(8,128)(2,1)S(1)}, u32[]{:S(2)}, u32[]{:S(2)}) collective-permute-start(bf16[1,128,3072]{2,1,0:T(8,128)(2,1)S(1)} %multiply_convert_fusion.cur_ref), channel_id=1, source_target_pairs={{0,1},{1,2},{2,3},{3,4},{4,5},{5,6},{6,7},{8,9},{9,10},{10,11},{11... | collective-permute-start | bytes 2359304 | tf_op jit(solution)/shard_map/ppermute | solution.py:137
  40.2 16.8 %collective-permute-start.1 = (f16[4,12,32,128]{3,2,1,0:T(8,128)(2,1)S(1)}, f16[4,12,32,128]{3,2,1,0:T(8,128)(2,1)S(1)}, u32[]{:S(2)}, u32[]{:S(2)}) collective-permute-start(f16[4,12,32,128]{3,2,1,0:T(8,128)(2,1)S(1)} %all-to-all-done.1), channel_id=1, source_target_pairs={{0,8},{8,0},{16,24},{24,16},{32,40},{40,32},{48,56},{56,48},{64,72... | collective-permute-start | bytes 1179656 | tf_op jit(solution)/shard_map/ppermute | solution.py:140
  56.8 1.0 %copy-start.2 = (bf16[512,256]{1,0:T(8,128)(2,1)S(1)}, bf16[512,256]{1,0:T(8,128)(2,1)}, u32[]{:S(2)}) copy-start(bf16[512,256]{1,0:T(8,128)(2,1)} %constant.27.clone.f_ref) | copy-start | bytes 786436
  56.9 1.0 %copy-start.3 = (bf16[256,256]{1,0:T(8,128)(2,1)S(1)}, bf16[256,256]{1,0:T(8,128)(2,1)}, u32[]{:S(2)}) copy-start(bf16[256,256]{1,0:T(8,128)(2,1)} %constant.28.clone.g_ref) | copy-start | bytes 393220

commit v8 on v7

v8 whole, which is shorter than its diff:
```python
import functools

import jax
import jax.numpy as jnp
import numpy as np
from jax import lax
from jax.experimental import pallas as pl
from jax.experimental.pallas import tpu as pltpu
from jax.sharding import PartitionSpec as P

WIRE = jnp.float16
SCALE = 4096.0

dot = functools.partial(jnp.dot, preferred_element_type=jnp.float32)
dot_rows = functools.partial(
    lax.dot_general, dimension_numbers=(((1,), (1,)), ((), ())), preferred_element_type=jnp.float32
)


def split(x):
    x = np.asarray(x, np.float32)
    hi = x.astype(jnp.bfloat16)
    return hi, (x - hi.astype(np.float32)).astype(jnp.bfloat16)


def transforms(taps):
    n = 2 * taps
    angle = 2 * np.pi * np.outer(np.arange(taps) + 0.5, np.arange(n)) / n
    forward = np.concatenate([np.cos(angle), -np.sin(angle)])
    fh, fl = split(forward)
    gh, gl = split(forward.T[taps:] / (taps * SCALE))
    head, tail = fh[:, :taps], fl[:, :taps]
    return (
        np.concatenate([head, tail], axis=1),
        np.concatenate([fh[:, taps:], fl[:, taps:]], axis=1),
        np.block([[head, head], [tail, np.zeros_like(tail)]]),
        np.concatenate([gh, gl], axis=0),
    )


NEAR = 4
CHUNKS = 3


def near_order(members):
    return [members // 2] + [i for i in range(members) if i != members // 2]


def far_order(members):
    rows = members // CHUNKS
    return sorted(range(members), key=lambda i: (-(i % CHUNKS), (i // CHUNKS - rows // 2) % rows))


def stage_groups(peers):
    index = np.arange(peers).reshape(-1, NEAR, 2)
    chunks = index.shape[0]
    far = [index[far_order(chunks), near, core].tolist() for near in range(NEAR) for core in range(2)]
    near = [index[chunk, near_order(NEAR), core].tolist() for chunk in range(chunks) for core in range(2)]
    return far, near


def twice(x):
    return jnp.concatenate([x, x], axis=0)


def spectrum_kernel(cur_ref, query_ref, f_ref, x_ref, kept_ref, cur, sems):
    pairs = ((cur_ref, cur), (query_ref, kept_ref))
    copies = [pltpu.make_async_copy(source, target, sems.at[i]) for i, (source, target) in enumerate(pairs)]
    for copy in copies:
        copy.start()
    copies[0].wait()
    x_ref[...] = dot(f_ref[...], twice(cur[0]))
    copies[1].wait()


BLOCKS = 2


def gate_kernel(odd_ref, x_ref, prev_ref, mine_ref, other_ref, query_ref, d_ref, f_ref, g_ref, out_ref, prev, sem):
    copy = pltpu.make_async_copy(prev_ref, prev, sem)
    copy.start()
    f32, bf16 = jnp.float32, jnp.bfloat16
    near, far, _, taps = mine_ref.shape
    odd = odd_ref[0] == 1
    copy.wait()
    for block in range(BLOCKS):
        members = range(block * far // BLOCKS, (block + 1) * far // BLOCKS)
        width = query_ref.shape[2] // BLOCKS
        at = slice(block * width, (block + 1) * width)
        pieces = []
        for i in range(near):
            i = near_order(near).index(i)
            for ref, twin in ((mine_ref, other_ref), (other_ref, mine_ref)):
                chosen = [far_order(far).index(j) for j in members]
                pieces.append(jnp.stack([jnp.where(odd, twin[i, j], ref[i, j]) for j in chosen]))
        w = jnp.concatenate(pieces, axis=1).reshape(-1, taps)
        wh = w.astype(bf16)
        wl = (w - wh.astype(f32)).astype(bf16)
        h = dot_rows(f_ref[...], jnp.concatenate([wh, wl], axis=1))
        h = h[: 2 * taps] + h[2 * taps :]
        x = x_ref[:, at] + dot(d_ref[...], twice(prev[0, :, at]))
        xr, xi, hr, hi = x[:taps], x[taps:], h[:taps], h[taps:]
        p = jnp.concatenate([xr * hr - xi * hi, xr * hi + xi * hr], axis=0)
        ph = p.astype(bf16)
        low = (p - ph.astype(f32)).astype(bf16)
        y = dot(g_ref[...], ph)
        y = y[:taps] + y[taps:] + dot(g_ref[:taps], low)
        out_ref[0, :, at] = (query_ref[0, :, at].astype(f32) * y).astype(out_ref.dtype)


VMEM = pl.BlockSpec(memory_space=pltpu.VMEM)
ANY = pl.BlockSpec(memory_space=pl.ANY)
PARAMS = pltpu.CompilerParams(vmem_limit_bytes=24 << 20)


def spectrum(cur, query, forward):
    x = jax.ShapeDtypeStruct((forward.shape[0], cur.shape[2]), jnp.float32)
    return pl.pallas_call(
        spectrum_kernel,
        in_specs=[ANY] * 2 + [VMEM],
        out_specs=[VMEM] * 2,
        out_shape=[x, jax.ShapeDtypeStruct(query.shape, query.dtype)],
        scratch_shapes=[pltpu.VMEM(cur.shape, cur.dtype), pltpu.SemaphoreType.DMA((2,))],
        compiler_params=PARAMS,
        name="spectrum",
    )(cur, query, forward)


def gate(odd, x, prev, mine, other, query, earlier, forward, inverse):
    return pl.pallas_call(
        gate_kernel,
        in_specs=[pl.BlockSpec(memory_space=pltpu.SMEM), VMEM, ANY] + [VMEM] * 6,
        out_specs=VMEM,
        out_shape=jax.ShapeDtypeStruct(query.shape, jnp.bfloat16),
        scratch_shapes=[pltpu.VMEM(prev.shape, prev.dtype), pltpu.SemaphoreType.DMA],
        compiler_params=PARAMS,
        name="gate",
    )(odd, x, prev, mine, other, query, earlier, forward, inverse)


def exchange(copies, groups):
    return lax.all_to_all(copies, "fsdp", 0, 0, axis_index_groups=groups, tiled=True)


def per_device(query_proj, key_proj, value_proj, filters):
    f32 = jnp.float32
    peers, steps = lax.axis_size("fsdp"), lax.axis_size("seq")
    earlier_dft, own_dft, taps_dft, inverse = transforms(filters.shape[1])
    far, near = stage_groups(peers)
    mine = (filters * SCALE).astype(WIRE)
    mine = exchange(jnp.broadcast_to(mine, (len(far[0]),) + mine.shape), far)
    mixed = (key_proj.astype(f32) * value_proj.astype(f32)).astype(jnp.bfloat16)
    earlier = lax.ppermute(mixed, "seq", [(i, i + 1) for i in range(steps - 1)])
    x, query = spectrum(mixed, query_proj, own_dft)
    mine = exchange(jnp.broadcast_to(mine, (NEAR,) + mine.shape), near)
    other = lax.ppermute(mine, "fsdp", [(i, i ^ 1) for i in range(peers)])
    mine = mine.astype(f32)
    odd = (lax.axis_index("fsdp") % 2).astype(jnp.int32).reshape(1)
    return gate(odd, x, earlier, mine, other.astype(f32), query, earlier_dft, taps_dft, inverse)


def solution(mesh):
    rows = P("fsdp", "seq", None)
    return jax.shard_map(
        per_device,
        mesh=mesh,
        in_specs=(rows, rows, rows, P("fsdp", None)),
        out_specs=rows,
        check_vma=False,
    )
```

time: 61.1 us -> 59.6 us (0.975)
  waiting for transfers between devices: 16.2 us -> 15.3 us
  local copies, waits for them, and re-layouts: 1.61 us -> 0.86 us
    ppermute x1, waiting for transfers between devices: 13.6 us -> 11.8 us  [per_device(): earlier = lax.ppermute(mixed, 'seq', [(i, i + 1) for i in range(steps - 1)])]
    ppermute x1, waiting for transfers between devices: 0.01 us -> 0.8 us  [per_device(): other = lax.ppermute(mine, 'fsdp', [(i, i ^ 1) for i in range(peers)])]
    unnamed x10 -> x12, local copies, waits for them, and re-layouts: 0.78 us -> 0.03 us
    pallas_call x1, Pallas kernels: 2.93 us -> 3.57 us  [gate(): pl.pallas_call(gate_kernel, in_specs=[pl.BlockSpec(memory_space=pltpu.SME...]
  transfers between devices with their start and end apart: 3 -> 3, of which waited for: 2 -> 3; matrix products, arithmetic and copies ran while one was open for 2% -> 3% of each run, Pallas kernels for 2% -> 1%
where the time goes in v8:
time: 59.6 us; the launch traced here: 59.2 us
  blocking collectives  24.9 us (42%)
  waiting for transfers between devices  15.3 us (26%)
  starting transfers between devices  11.5 us (19%)
  Pallas kernels  4.28 us (7%)
  other arithmetic  2.29 us (4%)
  local copies, waits for them, and re-layouts  0.86 us (1%)
    all_to_all x1, blocking collectives, exchange(): lax.all_to_all(copies, 'fsdp', 0, 0, axis_index_groups=groups, tiled=True)  24.9 us
    ppermute x1, waiting for transfers between devices, per_device(): earlier = lax.ppermute(mixed, 'seq', [(i, i + 1) for i in range(steps - 1)])  11.8 us
    all_to_all x1, starting transfers between devices, exchange(): lax.all_to_all(copies, 'fsdp', 0, 0, axis_index_groups=groups, tiled=True)  6.21 us
    pallas_call x1, Pallas kernels, gate(): pl.pallas_call(gate_kernel, in_specs=[pl.BlockSpec(memory_space=pltpu.SME...  3.57 us
    ppermute x1, starting transfers between devices, per_device(): earlier = lax.ppermute(mixed, 'seq', [(i, i + 1) for i in range(steps - 1)])  3.4 us
    all_to_all x1, waiting for transfers between devices, exchange(): lax.all_to_all(copies, 'fsdp', 0, 0, axis_index_groups=groups, tiled=True)  2.66 us
    ppermute x1, starting transfers between devices, per_device(): other = lax.ppermute(mine, 'fsdp', [(i, i ^ 1) for i in range(peers)])  1.91 us
    convert_element_type x1, other arithmetic, per_device(): mixed = (key_proj.astype(f32) * value_proj.astype(f32)).astype(jnp.bfloat16)  1.32 us
  transfers between devices with their start and end apart: 3, of which 3 were waited for; matrix products, arithmetic and copies ran while one was open for 3% of the time, Pallas kernels for 1%

profile of v8, /device:TPU:40, one launch (start us, length us, event | category | flops | bytes accessed | tf_op | source)
XLA Modules:
  0.0 59.2 jit_solution(9224517834430079344)
XLA Ops:
  0.0 0.0 copy-start.5
  0.0 0.8 %multiply_convert_fusion.1 = f16[32,128]{1,0:T(8,128)(2,1)S(1)} fusion(f32[32,128]{1,0:T(8,128)} %param.11), kind=kLoop, calls=%fused_computation.1 | loop fusion | flops 8192 | bytes 24576 | tf_op jit(solution)/shard_map/convert_element_type | solution.py:150
  0.8 24.9 %all_to_all.10 = f16[12,32,128]{2,1,0:T(8,128)(2,1)S(1)} all-to-all(f16[12,32,128]{2,1,0:T(8,128)(2,1)S(1)} %broadcast_in_dim.6), channel_id=1, replica_groups={{512,704,128,320,448,640,64,256,384,576,0,192},{520,712,136,328,456,648..., dimensions={0} | all-to-all | bytes 196608 | tf_op jit(solution)/shard_map/all_to_all | solution.py:142
  25.7 0.8 %broadcast_in_dim.7 = f16[4,12,32,128]{3,2,1,0:T(8,128)(2,1)} broadcast(f16[12,32,128]{2,1,0:T(8,128)(2,1)S(1)} %all_to_all.10), dimensions={1,2,3} | broadcast | bytes 491520 | tf_op jit(solution)/shard_map/broadcast_in_dim | solution.py:155
  26.6 6.2 %all-to-all-start.1 = ((f16[4,12,32,128]{3,2,1,0:T(8,128)(2,1)}), f16[4,12,32,128]{3,2,1,0:T(8,128)(2,1)S(1)}, u32[]{:S(2)}, u32[]{:S(2)}) async-start(f16[4,12,32,128]{3,2,1,0:T(8,128)(2,1)} %broadcast_in_dim.7), calls=%async_computation.1 | async-start | bytes 786432 | tf_op jit(solution)/shard_map/all_to_all | solution.py:142
  32.8 0.0 copy-done.5
  32.8 1.3 %multiply_convert_fusion.cur_ref = bf16[1,128,3072]{2,1,0:T(8,128)(2,1)S(1)} fusion(bf16[1,128,3072]{2,1,0:T(8,128)(2,1)S(1)} %copy-done.5, bf16[1,128,3072]{2,1,0:T(8,128)(2,1)} %param.9), kind=kLoop, calls=%fused_computation | loop fusion | flops 1572864 | bytes 2359296 | tf_op jit(solution)/shard_map/convert_element_type | solution.py:152
  34.1 3.4 %collective-permute-start = (bf16[1,128,3072]{2,1,0:T(8,128)(2,1)S(1)}, bf16[1,128,3072]{2,1,0:T(8,128)(2,1)S(1)}, u32[]{:S(2)}, u32[]{:S(2)}) collective-permute-start(bf16[1,128,3072]{2,1,0:T(8,128)(2,1)S(1)} %multiply_convert_fusion.cur_ref), channel_id=1, source_target_pairs={{0,1},{1,2},{2,3},{3,4},{4,5},{5,6},{6,7},{8,9},{9,10},{10,11},{11... | collective-permute-start | bytes 2359304 | tf_op jit(solution)/shard_map/ppermute | solution.py:153
  37.5 2.7 %all-to-all-done.1 = f16[4,12,32,128]{3,2,1,0:T(8,128)(2,1)S(1)} async-done(((f16[4,12,32,128]{3,2,1,0:T(8,128)(2,1)}), f16[4,12,32,128]{3,2,1,0:T(8,128)(2,1)S(1)}, u32[]{:S(2)}, u32[]{:S(2)}) %all-to-all-start.1) | async-done | bytes 393248 | tf_op jit(solution)/shard_map/all_to_all | solution.py:142
  40.2 1.9 %collective-permute-start.1 = (f16[4,12,32,128]{3,2,1,0:T(8,128)(2,1)S(1)}, f16[4,12,32,128]{3,2,1,0:T(8,128)(2,1)S(1)}, u32[]{:S(2)}, u32[]{:S(2)}) collective-permute-start(f16[4,12,32,128]{3,2,1,0:T(8,128)(2,1)S(1)} %all-to-all-done.1), channel_id=1, source_target_pairs={{0,8},{8,0},{16,24},{24,16},{32,40},{40,32},{48,56},{56,48},{64,72... | collective-permute-start | bytes 1179656 | tf_op jit(solution)/shard_map/ppermute | solution.py:156
  42.1 0.0 copy-done
  42.1 0.0 copy-done.4
  42.1 0.7 %spectrum.1 = (f32[256,3072]{1,0:T(8,128)S(1)}, bf16[1,128,3072]{2,1,0:T(8,128)(2,1)S(1)}) custom-call(bf16[1,128,3072]{2,1,0:T(8,128)(2,1)S(1)} %multiply_convert_fusion.cur_ref, bf16[1,128,3072]{2,1,0:T(8,128)(2,1)S(1)} %copy-done, bf16[256,256]{1,0:T(8,128)(2,1)S(1)} %copy-done.4), custom_call_target="tpu_custom_call" | custom-call | tf_op jit(solution)/shard_map/spectrum/pallas_call | solution.py:118
  42.8 0.0 copy-start.1
  42.8 0.0 copy-start.2
  42.9 0.0 copy-start.3
  42.9 0.1 convert_element_type.22.mine_ref
  43.0 0.8 %collective-permute-done.1 = f16[4,12,32,128]{3,2,1,0:T(8,128)(2,1)S(1)} collective-permute-done((f16[4,12,32,128]{3,2,1,0:T(8,128)(2,1)S(1)}, f16[4,12,32,128]{3,2,1,0:T(8,128)(2,1)S(1)}, u32[]{:S(2)}, u32[]{:S(2)}) %collective-permute-start.1) | collective-permute-done | bytes 393248 | tf_op jit(solution)/shard_map/ppermute | solution.py:156
  43.8 0.1 convert_element_type.23.other_ref
  43.9 11.8 %collective-permute-done.prev_ref = bf16[1,128,3072]{2,1,0:T(8,128)(2,1)S(1)} collective-permute-done((bf16[1,128,3072]{2,1,0:T(8,128)(2,1)S(1)}, bf16[1,128,3072]{2,1,0:T(8,128)(2,1)S(1)}, u32[]{:S(2)}, u32[]{:S(2)}) %collective-permute-start) | collective-permute-done | bytes 786464 | tf_op jit(solution)/shard_map/ppermute | solution.py:153
  55.7 0.0 copy-done.1
  55.7 0.0 copy-done.2
  55.7 0.0 copy-done.3
  55.7 3.6 %gate.1 = bf16[1,128,3072]{2,1,0:T(8,128)(2,1)} custom-call(s32[1]{0:T(128)} %bitcast.odd_ref, f32[256,3072]{1,0:T(8,128)S(1)} %get-tuple-element.7.x_ref, bf16[1,128,3072]{2,1,0:T(8,128)(2,1)S(1)} %collective-permute-done.prev_ref, f32[4,12,32,128]{3,2,1,0:T(8,128)S(1)} %convert_element_type.22.mine_ref, ...), custom_call_target="tpu_custom_call" | custom-call | tf_op jit(solution)/shard_map/gate/pallas_call | solution.py:130
  (3 shorter events, 0.0 us)
Async XLA Ops:
  0.0 32.8 %copy-start.5 = (bf16[1,128,3072]{2,1,0:T(8,128)(2,1)S(1)}, bf16[1,128,3072]{2,1,0:T(8,128)(2,1)}, u32[]{:S(2)}) copy-start(bf16[1,128,3072]{2,1,0:T(8,128)(2,1)} %param.10) | copy-start | bytes 2359300
  26.6 15.5 %copy-start = (bf16[1,128,3072]{2,1,0:T(8,128)(2,1)S(1)}, bf16[1,128,3072]{2,1,0:T(8,128)(2,1)}, u32[]{:S(2)}) copy-start(bf16[1,128,3072]{2,1,0:T(8,128)(2,1)} %query_ref.1) | copy-start | bytes 2359300
  26.6 15.6 %copy-start.4 = (bf16[256,256]{1,0:T(8,128)(2,1)S(1)}, bf16[256,256]{1,0:T(8,128)(2,1)}, u32[]{:S(2)}) copy-start(bf16[256,256]{1,0:T(8,128)(2,1)} %constant.28.clone.f_ref) | copy-start | bytes 393220
  26.6 13.6 %all-to-all-start.1 = ((f16[4,12,32,128]{3,2,1,0:T(8,128)(2,1)}), f16[4,12,32,128]{3,2,1,0:T(8,128)(2,1)S(1)}, u32[]{:S(2)}, u32[]{:S(2)}) async-start(f16[4,12,32,128]{3,2,1,0:T(8,128)(2,1)} %broadcast_in_dim.7), calls=%async_computation.1 | async-start | bytes 786432 | tf_op jit(solution)/shard_map/all_to_all | solution.py:142
  34.1 21.6 %collective-permute-start = (bf16[1,128,3072]{2,1,0:T(8,128)(2,1)S(1)}, bf16[1,128,3072]{2,1,0:T(8,128)(2,1)S(1)}, u32[]{:S(2)}, u32[]{:S(2)}) collective-permute-start(bf16[1,128,3072]{2,1,0:T(8,128)(2,1)S(1)} %multiply_convert_fusion.cur_ref), channel_id=1, source_target_pairs={{0,1},{1,2},{2,3},{3,4},{4,5},{5,6},{6,7},{8,9},{9,10},{10,11},{11... | collective-permute-start | bytes 2359304 | tf_op jit(solution)/shard_map/ppermute | solution.py:153
  40.2 3.6 %collective-permute-start.1 = (f16[4,12,32,128]{3,2,1,0:T(8,128)(2,1)S(1)}, f16[4,12,32,128]{3,2,1,0:T(8,128)(2,1)S(1)}, u32[]{:S(2)}, u32[]{:S(2)}) collective-permute-start(f16[4,12,32,128]{3,2,1,0:T(8,128)(2,1)S(1)} %all-to-all-done.1), channel_id=1, source_target_pairs={{0,8},{8,0},{16,24},{24,16},{32,40},{40,32},{48,56},{56,48},{64,72... | collective-permute-start | bytes 1179656 | tf_op jit(solution)/shard_map/ppermute | solution.py:156
  42.8 12.8 %copy-start.1 = (bf16[512,256]{1,0:T(8,128)(2,1)S(1)}, bf16[512,256]{1,0:T(8,128)(2,1)}, u32[]{:S(2)}) copy-start(bf16[512,256]{1,0:T(8,128)(2,1)} %constant.30.clone.f_ref) | copy-start | bytes 786436
  42.8 12.8 %copy-start.2 = (bf16[256,256]{1,0:T(8,128)(2,1)S(1)}, bf16[256,256]{1,0:T(8,128)(2,1)}, u32[]{:S(2)}) copy-start(bf16[256,256]{1,0:T(8,128)(2,1)} %constant.29.clone.d_ref) | copy-start | bytes 393220
  42.9 12.8 %copy-start.3 = (bf16[256,256]{1,0:T(8,128)(2,1)S(1)}, bf16[256,256]{1,0:T(8,128)(2,1)}, u32[]{:S(2)}) copy-start(bf16[256,256]{1,0:T(8,128)(2,1)} %constant.31.clone.g_ref) | copy-start | bytes 393220
